TPU v7x, 128 devices: a whole 4x4x4 slice. The times are simulated.
128 devices in a mesh: row: 8 (over y_lo, z), col: 16 (over y_hi, x, core).
Axes of the slice: x: 4, y: 4 (y_hi: 2, y_lo: 2; y = y_hi * 2 + y_lo), z: 4, core: 2. Of those that a mesh axis runs over, the one named last changes fastest.
Arguments:
- block_values: bfloat16 [32, 16, 256, 256], P('row', 'col'), may hold values from -0.625 to 0.625
- block_columns: int32 [32, 16], P('row', 'col'), may hold values from 0 to 1
- block_live: int32 [32, 16], P('row', 'col'), may hold values 0 or 1
Outputs:
- updated: bfloat16 [32, 16, 256, 256], P('row', 'col')
All inputs are finite; a program needn't handle non-finite values. No bound on the sum of `block_live` on one device may be relied on, other than what follows from the above.
Results may differ from a plain program's by a relative error of at most 0.0048.
Values may be sent and summed in bfloat16 or wider, within the bound.
A program may use at most 128 MiB of HBM per device.

v0:
```python
import jax
import jax.numpy as jnp
from jax import lax
from jax.sharding import PartitionSpec as P


def from_root(block, axis, owner):
    block = jnp.where(lax.axis_index(axis) == owner, block, jnp.zeros_like(block))
    return lax.psum(block, axis)


def shifted(value, axis, by):
    count = lax.axis_size(axis)
    return lax.ppermute(value, axis, [(i, (i + by) % count) for i in range(count)])


def select_blocks(right_values, right_columns, position, own_columns, live_now):
    chosen = jnp.take(right_values, position, axis=0)
    chosen_columns = jnp.take(right_columns, position, axis=0)
    weight = ((chosen_columns == own_columns[:, None]) & (live_now[:, None] > 0)).astype(
        jnp.bfloat16
    )
    return chosen * weight[:, :, None, None]


def body(block_values, block_columns, block_live):
    row_count = lax.axis_size("row")
    column_ratio = lax.axis_size("col") // row_count
    local_rows = block_values.shape[0]
    block_width = block_values.shape[2]
    group_width = local_rows // column_ratio
    own_columns = block_columns[:, 0]
    live_now = block_live[:, 0]
    masked = block_values * block_live[:, :, None, None].astype(jnp.bfloat16)
    column_wire = block_columns.astype(jnp.bfloat16)
    row_position = lax.axis_index("row")

    def multiply(right_side):
        running = jnp.zeros((local_rows, block_width, block_width), jnp.float32)
        pieces = (right_side, column_wire)
        for turn_index in range(row_count):
            source_group = (row_position - turn_index) % row_count
            for part_index in range(column_ratio):
                owner_column = source_group * column_ratio + part_index
                left_values, left_columns = (
                    from_root(masked, "col", owner_column),
                    from_root(column_wire, "col", owner_column),
                )
                position = part_index * group_width + left_columns.astype(jnp.int32)
                chosen = select_blocks(
                    pieces[0][:, 0],
                    pieces[1][:, 0].astype(jnp.int32),
                    position,
                    own_columns,
                    live_now,
                )
                running = running + jnp.einsum(
                    "ijxy,ijyz->ixz", left_values, chosen, preferred_element_type=jnp.float32
                )
            if turn_index + 1 < row_count:
                pieces = shifted((pieces[0], pieces[1]), "row", 1)
        return running

    squared = multiply(masked).astype(jnp.bfloat16)[:, None]
    cube_part = multiply(squared)
    updated = 1.5 * masked[:, 0].astype(jnp.float32) - 0.5 * cube_part
    return updated.astype(jnp.bfloat16)[:, None]


def solution(mesh):
    return jax.shard_map(
        body,
        mesh=mesh,
        in_specs=(P("row", "col", None, None), P("row", "col"), P("row", "col")),
        out_specs=P("row", "col", None, None),
        check_vma=False,
    )
```

profile of v0, /device:TPU:0, one launch (start us, length us, event | category | flops | bytes accessed | tf_op | source)
XLA Modules:
  0.0 384.6 jit_solution(8846536334471375172)
XLA Ops:
  7.2 2.0 select_bitcast_fusion
  9.2 3.2 select_bitcast_fusion.1
  12.4 2.1 collective-permute-start
  14.4 1.9 collective-permute-start.1
  16.4 38.2 %all-reduce = (bf16[4,1]{0,1:T(2,128)(2,1)S(1)}, bf16[4,1]{0,1:T(2,128)(2,1)S(1)}, bf16[4,1]{0,1:T(2,128)(2,1)S(1)}, bf16[4,1]{0,1:T(2,128)(2,1)S(1)}, bf16[4,1]...) all-reduce(bf16[4,1]{0,1:T(2,128)(2,1)S(1)} %get-tuple-element.91, ...), channel_id=1, replica_groups=mesh['row'=8,'col'=16] {'col'}, use_global_device_ids=true, to_apply=%region_1.2 | all-reduce | flops 64 | bytes 256 | tf_op jit(solution)/shard_map/psum | solution.py:9
  58.8 1.6 collective-permute-start.2
  60.5 26.9 %collective-permute-done.2 = bf16[4,1,256,256]{3,2,0,1:T(8,128)(2,1)S(1)} collective-permute-done((bf16[4,1,256,256]{3,2,0,1:T(8,128)(2,1)S(1)}, bf16[4,1,256,256]{3,2,0,1:T(8,128)(2,1)S(1)}, u32[]{:S(2)}, u32[]{:S(2)}) %collective-permute-start.2) | collective-permute-done | bytes 524320 | tf_op jit(solution)/shard_map/ppermute | solution.py:14
  87.4 19.9 %collective-permute-done.4 = bf16[4,1,256,256]{3,2,0,1:T(8,128)(2,1)S(1)} collective-permute-done((bf16[4,1,256,256]{3,2,0,1:T(8,128)(2,1)S(1)}, bf16[4,1,256,256]{3,2,0,1:T(8,128)(2,1)S(1)}, u32[]{:S(2)}, u32[]{:S(2)}) %collective-permute-start.4) | collective-permute-done | bytes 524320 | tf_op jit(solution)/shard_map/ppermute | solution.py:14
  107.4 31.5 %collective-permute-done.6 = bf16[4,1,256,256]{3,2,0,1:T(8,128)(2,1)S(1)} collective-permute-done((bf16[4,1,256,256]{3,2,0,1:T(8,128)(2,1)S(1)}, bf16[4,1,256,256]{3,2,0,1:T(8,128)(2,1)S(1)}, u32[]{:S(2)}, u32[]{:S(2)}) %collective-permute-start.6) | collective-permute-done | bytes 524320 | tf_op jit(solution)/shard_map/ppermute | solution.py:14
  140.1 33.5 %collective-permute-done.3 = bf16[4,1]{0,1:T(2,128)(2,1)S(1)} collective-permute-done((bf16[4,1]{0,1:T(2,128)(2,1)S(1)}, bf16[4,1]{0,1:T(2,128)(2,1)S(1)}, u32[]{:S(2)}, u32[]{:S(2)}) %collective-permute-start.3) | collective-permute-done | bytes 40 | tf_op jit(solution)/shard_map/ppermute | solution.py:14
  175.0 6.5 %collective-permute-done.5 = bf16[4,1]{0,1:T(2,128)(2,1)S(1)} collective-permute-done((bf16[4,1]{0,1:T(2,128)(2,1)S(1)}, bf16[4,1]{0,1:T(2,128)(2,1)S(1)}, u32[]{:S(2)}, u32[]{:S(2)}) %collective-permute-start.5) | collective-permute-done | bytes 40 | tf_op jit(solution)/shard_map/ppermute | solution.py:14
  182.9 5.5 %collective-permute-done.7 = bf16[4,1]{0,1:T(2,128)(2,1)S(1)} collective-permute-done((bf16[4,1]{0,1:T(2,128)(2,1)S(1)}, bf16[4,1]{0,1:T(2,128)(2,1)S(1)}, u32[]{:S(2)}, u32[]{:S(2)}) %collective-permute-start.7) | collective-permute-done | bytes 40 | tf_op jit(solution)/shard_map/ppermute | solution.py:14
  189.7 5.6 %collective-permute-done.9 = bf16[4,1]{0,1:T(2,128)(2,1)S(1)} collective-permute-done((bf16[4,1]{0,1:T(2,128)(2,1)S(1)}, bf16[4,1]{0,1:T(2,128)(2,1)S(1)}, u32[]{:S(2)}, u32[]{:S(2)}) %collective-permute-start.9) | collective-permute-done | bytes 40 | tf_op jit(solution)/shard_map/ppermute | solution.py:14
  196.7 5.7 %collective-permute-done.11 = bf16[4,1]{0,1:T(2,128)(2,1)S(1)} collective-permute-done((bf16[4,1]{0,1:T(2,128)(2,1)S(1)}, bf16[4,1]{0,1:T(2,128)(2,1)S(1)}, u32[]{:S(2)}, u32[]{:S(2)}) %collective-permute-start.11) | collective-permute-done | bytes 40 | tf_op jit(solution)/shard_map/ppermute | solution.py:14
  204.0 5.4 %collective-permute-done.13 = bf16[4,1]{0,1:T(2,128)(2,1)S(1)} collective-permute-done((bf16[4,1]{0,1:T(2,128)(2,1)S(1)}, bf16[4,1]{0,1:T(2,128)(2,1)S(1)}, u32[]{:S(2)}, u32[]{:S(2)}) %collective-permute-start.13) | collective-permute-done | bytes 40 | tf_op jit(solution)/shard_map/ppermute | solution.py:14
  224.4 1.6 gather_fusion.24
  226.1 1.6 gather_fusion.26
  227.7 1.6 gather_fusion.28
  229.3 1.7 gather_fusion.30
  252.7 13.8 %collective-permute-done.14 = bf16[4,1,256,256]{3,2,0,1:T(8,128)(2,1)S(1)} collective-permute-done((bf16[4,1,256,256]{3,2,0,1:T(8,128)(2,1)S(1)}, bf16[4,1,256,256]{3,2,0,1:T(8,128)(2,1)S(1)}, u32[]{:S(2)}, u32[]{:S(2)}) %collective-permute-start.14) | collective-permute-done | bytes 524320 | tf_op jit(solution)/shard_map/ppermute | solution.py:14
  269.4 1.7 convolution_add_fusion.13
  271.4 15.0 %collective-permute-done.15 = bf16[4,1,256,256]{3,2,0,1:T(8,128)(2,1)S(1)} collective-permute-done((bf16[4,1,256,256]{3,2,0,1:T(8,128)(2,1)}, bf16[4,1,256,256]{3,2,0,1:T(8,128)(2,1)S(1)}, u32[]{:S(2)}, u32[]{:S(2)}) %collective-permute-start.15) | collective-permute-done | bytes 524320 | tf_op jit(solution)/shard_map/ppermute | solution.py:14
  289.1 1.7 convolution_add_fusion.11
  291.2 14.0 %collective-permute-done.16 = bf16[4,1,256,256]{3,2,0,1:T(8,128)(2,1)S(1)} collective-permute-done((bf16[4,1,256,256]{3,2,0,1:T(8,128)(2,1)S(1)}, bf16[4,1,256,256]{3,2,0,1:T(8,128)(2,1)S(1)}, u32[]{:S(2)}, u32[]{:S(2)}) %collective-permute-start.16) | collective-permute-done | bytes 524320 | tf_op jit(solution)/shard_map/ppermute | solution.py:14
  308.0 1.7 convolution_add_fusion.9
  310.0 13.1 %collective-permute-done.17 = bf16[4,1,256,256]{3,2,0,1:T(8,128)(2,1)S(1)} collective-permute-done((bf16[4,1,256,256]{3,2,0,1:T(8,128)(2,1)S(1)}, bf16[4,1,256,256]{3,2,0,1:T(8,128)(2,1)S(1)}, u32[]{:S(2)}, u32[]{:S(2)}) %collective-permute-start.17) | collective-permute-done | bytes 524320 | tf_op jit(solution)/shard_map/ppermute | solution.py:14
  325.9 1.7 convolution_add_fusion.7
  328.0 12.2 %collective-permute-done.18 = bf16[4,1,256,256]{3,2,0,1:T(8,128)(2,1)S(1)} collective-permute-done((bf16[4,1,256,256]{3,2,0,1:T(8,128)(2,1)S(1)}, bf16[4,1,256,256]{3,2,0,1:T(8,128)(2,1)S(1)}, u32[]{:S(2)}, u32[]{:S(2)}) %collective-permute-start.18) | collective-permute-done | bytes 524320 | tf_op jit(solution)/shard_map/ppermute | solution.py:14
  342.9 1.7 convolution_add_fusion.5
  345.0 11.3 %collective-permute-done.19 = bf16[4,1,256,256]{3,2,0,1:T(8,128)(2,1)S(1)} collective-permute-done((bf16[4,1,256,256]{3,2,0,1:T(8,128)(2,1)S(1)}, bf16[4,1,256,256]{3,2,0,1:T(8,128)(2,1)S(1)}, u32[]{:S(2)}, u32[]{:S(2)}) %collective-permute-start.19) | collective-permute-done | bytes 524320 | tf_op jit(solution)/shard_map/ppermute | solution.py:14
  361.0 9.4 %collective-permute-done.20 = bf16[4,1,256,256]{3,2,0,1:T(8,128)(2,1)S(1)} collective-permute-done((bf16[4,1,256,256]{3,2,0,1:T(8,128)(2,1)S(1)}, bf16[4,1,256,256]{3,2,0,1:T(8,128)(2,1)S(1)}, u32[]{:S(2)}, u32[]{:S(2)}) %collective-permute-start.20) | collective-permute-done | bytes 524320 | tf_op jit(solution)/shard_map/ppermute | solution.py:14
  371.1 2.5 gather_fusion.46
  (232 shorter events, 74.7 us)
Async XLA Ops:
  6.5 224.5 %all-reduce.4.cloned.1.call-start = ((), (), s32[]{:S(2)}) async-start(), calls=%async_computation | async-start | bytes 16777216 | tf_op jit(solution)/shard_map/psum | solution.py:9
  12.3 2.1 copy-start.48
  12.4 46.4 %collective-permute-start = (bf16[4,1,256,256]{3,2,0,1:T(8,128)(2,1)S(1)}, bf16[4,1,256,256]{3,2,0,1:T(8,128)(2,1)S(1)}, u32[]{:S(2)}, u32[]{:S(2)}) collective-permute-start(bf16[4,1,256,256]{3,2,0,1:T(8,128)(2,1)S(1)} %get-tuple-element.40), channel_id=1, source_target_pairs={{0,16},{16,32},{32,48},{48,64},{64,80},{80,96},{96,112},{112,0},{1... | collective-permute-start | bytes 1572872 | tf_op jit(solution)/shard_map/ppermute | solution.py:14
  14.4 124.4 %collective-permute-start.1 = (bf16[4,1]{0,1:T(2,128)(2,1)S(1)}, bf16[4,1]{0,1:T(2,128)(2,1)S(1)}, u32[]{:S(2)}, u32[]{:S(2)}) collective-permute-start(bf16[4,1]{0,1:T(2,128)(2,1)S(1)} %get-tuple-element.88), channel_id=1, source_target_pairs={{0,16},{16,32},{32,48},{48,64},{64,80},{80,96},{96,112},{112,0},{1... | collective-permute-start | bytes 32 | tf_op jit(solution)/shard_map/ppermute | solution.py:14
  58.8 28.6 %collective-permute-start.2 = (bf16[4,1,256,256]{3,2,0,1:T(8,128)(2,1)S(1)}, bf16[4,1,256,256]{3,2,0,1:T(8,128)(2,1)S(1)}, u32[]{:S(2)}, u32[]{:S(2)}) collective-permute-start(bf16[4,1,256,256]{3,2,0,1:T(8,128)(2,1)S(1)} %collective-permute-done), channel_id=1, source_target_pairs={{0,16},{16,32},{32,48},{48,64},{64,80},{80,96},{96,112},{112,0},{1... | collective-permute-start | bytes 1572872 | tf_op jit(solution)/shard_map/ppermute | solution.py:14
  87.4 20.0 %collective-permute-start.4 = (bf16[4,1,256,256]{3,2,0,1:T(8,128)(2,1)S(1)}, bf16[4,1,256,256]{3,2,0,1:T(8,128)(2,1)S(1)}, u32[]{:S(2)}, u32[]{:S(2)}) collective-permute-start(bf16[4,1,256,256]{3,2,0,1:T(8,128)(2,1)S(1)} %collective-permute-done.2), channel_id=1, source_target_pairs={{0,16},{16,32},{32,48},{48,64},{64,80},{80,96},{96,112},{112,0},{1... | collective-permute-start | bytes 1572872 | tf_op jit(solution)/shard_map/ppermute | solution.py:14
  107.3 31.5 %collective-permute-start.6 = (bf16[4,1,256,256]{3,2,0,1:T(8,128)(2,1)S(1)}, bf16[4,1,256,256]{3,2,0,1:T(8,128)(2,1)S(1)}, u32[]{:S(2)}, u32[]{:S(2)}) collective-permute-start(bf16[4,1,256,256]{3,2,0,1:T(8,128)(2,1)S(1)} %collective-permute-done.4), channel_id=1, source_target_pairs={{0,16},{16,32},{32,48},{48,64},{64,80},{80,96},{96,112},{112,0},{1... | collective-permute-start | bytes 1572872 | tf_op jit(solution)/shard_map/ppermute | solution.py:14
  138.8 44.0 %collective-permute-start.8 = (bf16[4,1,256,256]{3,2,0,1:T(8,128)(2,1)S(1)}, bf16[4,1,256,256]{3,2,0,1:T(8,128)(2,1)S(1)}, u32[]{:S(2)}, u32[]{:S(2)}) collective-permute-start(bf16[4,1,256,256]{3,2,0,1:T(8,128)(2,1)S(1)} %collective-permute-done.6), channel_id=1, source_target_pairs={{0,16},{16,32},{32,48},{48,64},{64,80},{80,96},{96,112},{112,0},{1... | collective-permute-start | bytes 1572872 | tf_op jit(solution)/shard_map/ppermute | solution.py:14
  140.1 33.5 %collective-permute-start.3 = (bf16[4,1]{0,1:T(2,128)(2,1)S(1)}, bf16[4,1]{0,1:T(2,128)(2,1)S(1)}, u32[]{:S(2)}, u32[]{:S(2)}) collective-permute-start(bf16[4,1]{0,1:T(2,128)(2,1)S(1)} %collective-permute-done.1), channel_id=1, source_target_pairs={{0,16},{16,32},{32,48},{48,64},{64,80},{80,96},{96,112},{112,0},{1... | collective-permute-start | bytes 32 | tf_op jit(solution)/shard_map/ppermute | solution.py:14
  175.0 6.5 %collective-permute-start.5 = (bf16[4,1]{0,1:T(2,128)(2,1)S(1)}, bf16[4,1]{0,1:T(2,128)(2,1)S(1)}, u32[]{:S(2)}, u32[]{:S(2)}) collective-permute-start(bf16[4,1]{0,1:T(2,128)(2,1)S(1)} %collective-permute-done.3), channel_id=1, source_target_pairs={{0,16},{16,32},{32,48},{48,64},{64,80},{80,96},{96,112},{112,0},{1... | collective-permute-start | bytes 32 | tf_op jit(solution)/shard_map/ppermute | solution.py:14
  182.8 5.7 %collective-permute-start.7 = (bf16[4,1]{0,1:T(2,128)(2,1)S(1)}, bf16[4,1]{0,1:T(2,128)(2,1)S(1)}, u32[]{:S(2)}, u32[]{:S(2)}) collective-permute-start(bf16[4,1]{0,1:T(2,128)(2,1)S(1)} %collective-permute-done.5), channel_id=1, source_target_pairs={{0,16},{16,32},{32,48},{48,64},{64,80},{80,96},{96,112},{112,0},{1... | collective-permute-start | bytes 32 | tf_op jit(solution)/shard_map/ppermute | solution.py:14
  182.8 20.9 %collective-permute-start.10 = (bf16[4,1,256,256]{3,2,0,1:T(8,128)(2,1)S(1)}, bf16[4,1,256,256]{3,2,0,1:T(8,128)(2,1)}, u32[]{:S(2)}, u32[]{:S(2)}) collective-permute-start(bf16[4,1,256,256]{3,2,0,1:T(8,128)(2,1)S(1)} %collective-permute-done.8), channel_id=1, source_target_pairs={{0,16},{16,32},{32,48},{48,64},{64,80},{80,96},{96,112},{112,0},{1... | collective-permute-start | bytes 1572872 | tf_op jit(solution)/shard_map/ppermute | solution.py:14
  189.7 5.7 %collective-permute-start.9 = (bf16[4,1]{0,1:T(2,128)(2,1)S(1)}, bf16[4,1]{0,1:T(2,128)(2,1)S(1)}, u32[]{:S(2)}, u32[]{:S(2)}) collective-permute-start(bf16[4,1]{0,1:T(2,128)(2,1)S(1)} %collective-permute-done.7), channel_id=1, source_target_pairs={{0,16},{16,32},{32,48},{48,64},{64,80},{80,96},{96,112},{112,0},{1... | collective-permute-start | bytes 32 | tf_op jit(solution)/shard_map/ppermute | solution.py:14
  196.7 5.7 %collective-permute-start.11 = (bf16[4,1]{0,1:T(2,128)(2,1)S(1)}, bf16[4,1]{0,1:T(2,128)(2,1)S(1)}, u32[]{:S(2)}, u32[]{:S(2)}) collective-permute-start(bf16[4,1]{0,1:T(2,128)(2,1)S(1)} %collective-permute-done.9), channel_id=1, source_target_pairs={{0,16},{16,32},{32,48},{48,64},{64,80},{80,96},{96,112},{112,0},{1... | collective-permute-start | bytes 32 | tf_op jit(solution)/shard_map/ppermute | solution.py:14
  203.7 5.7 %collective-permute-start.13 = (bf16[4,1]{0,1:T(2,128)(2,1)S(1)}, bf16[4,1]{0,1:T(2,128)(2,1)S(1)}, u32[]{:S(2)}, u32[]{:S(2)}) collective-permute-start(bf16[4,1]{0,1:T(2,128)(2,1)S(1)} %collective-permute-done.11), channel_id=1, source_target_pairs={{0,16},{16,32},{32,48},{48,64},{64,80},{80,96},{96,112},{112,0},{1... | collective-permute-start | bytes 32 | tf_op jit(solution)/shard_map/ppermute | solution.py:14
  203.7 24.0 %collective-permute-start.12 = (bf16[4,1,256,256]{3,2,0,1:T(8,128)(2,1)}, bf16[4,1,256,256]{3,2,0,1:T(8,128)(2,1)}, u32[]{:S(2)}, u32[]{:S(2)}) collective-permute-start(bf16[4,1,256,256]{3,2,0,1:T(8,128)(2,1)} %collective-permute-done.10), channel_id=1, source_target_pairs={{0,16},{16,32},{32,48},{48,64},{64,80},{80,96},{96,112},{112,0},{1... | collective-permute-start | bytes 1572872 | tf_op jit(solution)/shard_map/ppermute | solution.py:14
  229.3 1.7 copy-start.28
  251.1 15.4 %collective-permute-start.14 = (bf16[4,1,256,256]{3,2,0,1:T(8,128)(2,1)S(1)}, bf16[4,1,256,256]{3,2,0,1:T(8,128)(2,1)S(1)}, u32[]{:S(2)}, u32[]{:S(2)}) collective-permute-start(bf16[4,1,256,256]{3,2,0,1:T(8,128)(2,1)S(1)} %bitcast.644), channel_id=1, source_target_pairs={{0,16},{16,32},{32,48},{48,64},{64,80},{80,96},{96,112},{112,0},{1... | collective-permute-start | bytes 1572872 | tf_op jit(solution)/shard_map/ppermute | solution.py:14
  269.3 1.7 copy-start.40
  269.3 17.0 %collective-permute-start.15 = (bf16[4,1,256,256]{3,2,0,1:T(8,128)(2,1)}, bf16[4,1,256,256]{3,2,0,1:T(8,128)(2,1)S(1)}, u32[]{:S(2)}, u32[]{:S(2)}) collective-permute-start(bf16[4,1,256,256]{3,2,0,1:T(8,128)(2,1)} %copy-done.1), channel_id=1, source_target_pairs={{0,16},{16,32},{32,48},{48,64},{64,80},{80,96},{96,112},{112,0},{1... | collective-permute-start | bytes 1572872 | tf_op jit(solution)/shard_map/ppermute | solution.py:14
  289.1 1.7 copy-start.20
  289.1 1.7 copy-start.41
  289.1 16.1 %collective-permute-start.16 = (bf16[4,1,256,256]{3,2,0,1:T(8,128)(2,1)S(1)}, bf16[4,1,256,256]{3,2,0,1:T(8,128)(2,1)S(1)}, u32[]{:S(2)}, u32[]{:S(2)}) collective-permute-start(bf16[4,1,256,256]{3,2,0,1:T(8,128)(2,1)S(1)} %collective-permute-done.15), channel_id=1, source_target_pairs={{0,16},{16,32},{32,48},{48,64},{64,80},{80,96},{96,112},{112,0},{1... | collective-permute-start | bytes 1572872 | tf_op jit(solution)/shard_map/ppermute | solution.py:14
  308.0 1.7 copy-start.42
  308.0 15.2 %collective-permute-start.17 = (bf16[4,1,256,256]{3,2,0,1:T(8,128)(2,1)S(1)}, bf16[4,1,256,256]{3,2,0,1:T(8,128)(2,1)S(1)}, u32[]{:S(2)}, u32[]{:S(2)}) collective-permute-start(bf16[4,1,256,256]{3,2,0,1:T(8,128)(2,1)S(1)} %collective-permute-done.16), channel_id=1, source_target_pairs={{0,16},{16,32},{32,48},{48,64},{64,80},{80,96},{96,112},{112,0},{1... | collective-permute-start | bytes 1572872 | tf_op jit(solution)/shard_map/ppermute | solution.py:14
  325.9 1.7 copy-start.14
  325.9 1.7 copy-start.43
  325.9 14.3 %collective-permute-start.18 = (bf16[4,1,256,256]{3,2,0,1:T(8,128)(2,1)S(1)}, bf16[4,1,256,256]{3,2,0,1:T(8,128)(2,1)S(1)}, u32[]{:S(2)}, u32[]{:S(2)}) collective-permute-start(bf16[4,1,256,256]{3,2,0,1:T(8,128)(2,1)S(1)} %collective-permute-done.17), channel_id=1, source_target_pairs={{0,16},{16,32},{32,48},{48,64},{64,80},{80,96},{96,112},{112,0},{1... | collective-permute-start | bytes 1572872 | tf_op jit(solution)/shard_map/ppermute | solution.py:14
  342.9 1.7 copy-start.44
  342.9 13.4 %collective-permute-start.19 = (bf16[4,1,256,256]{3,2,0,1:T(8,128)(2,1)S(1)}, bf16[4,1,256,256]{3,2,0,1:T(8,128)(2,1)S(1)}, u32[]{:S(2)}, u32[]{:S(2)}) collective-permute-start(bf16[4,1,256,256]{3,2,0,1:T(8,128)(2,1)S(1)} %collective-permute-done.18), channel_id=1, source_target_pairs={{0,16},{16,32},{32,48},{48,64},{64,80},{80,96},{96,112},{112,0},{1... | collective-permute-start | bytes 1572872 | tf_op jit(solution)/shard_map/ppermute | solution.py:14
  359.0 11.3 %collective-permute-start.20 = (bf16[4,1,256,256]{3,2,0,1:T(8,128)(2,1)S(1)}, bf16[4,1,256,256]{3,2,0,1:T(8,128)(2,1)S(1)}, u32[]{:S(2)}, u32[]{:S(2)}) collective-permute-start(bf16[4,1,256,256]{3,2,0,1:T(8,128)(2,1)S(1)} %collective-permute-done.19), channel_id=1, source_target_pairs={{0,16},{16,32},{32,48},{48,64},{64,80},{80,96},{96,112},{112,0},{1... | collective-permute-start | bytes 1572872 | tf_op jit(solution)/shard_map/ppermute | solution.py:14
  371.1 2.5 copy-start.3
  (40 other events, 48.4 us)
Sparse Core Ops, SparseCore 0:
  12.5 168.7 all-reduce.3
where the time goes:
time: 386 us; the launch traced here: 385 us
  waiting for transfers between devices  229 us (59%)
  local copies, waits for them, and re-layouts  68.7 us (18%)
  blocking collectives  38.2 us (10%)
  matrix products  22.5 us (6%)
  between operations  14.2 us (4%)
  starting transfers between devices  6.01 us (2%)
  other arithmetic  5.42 us (1%)
    ppermute x21, waiting for transfers between devices, shifted(): lax.ppermute(value, axis, [(i, (i + by) % count) for i in range(count)])  229 us
    gather x32, local copies, waits for them, and re-layouts, select_blocks(): chosen = jnp.take(right_values, position, axis=0)  45.4 us
    psum x1, blocking collectives, from_root(): return lax.psum(block, axis)  38.2 us
    dot_general x32, matrix products, multiply(): jnp.einsum('ijxy,ijyz->ixz', left_values, chosen, preferred_element_type=...  22.5 us
    unnamed x100, local copies, waits for them, and re-layouts  13.1 us
    gather x16, local copies, waits for them, and re-layouts, select_blocks(): chosen_columns = jnp.take(right_columns, position, axis=0)  10.2 us
  transfers between devices with their start and end apart: 22, of which 16 were waited for; matrix products, arithmetic and copies ran while one was open for 12% of the time, Pallas kernels for 0%

commit v1 on v0

v1 whole, which is shorter than its diff:
```python
import functools

import jax
import jax.numpy as jnp
from jax import lax
from jax.experimental import pallas as pl
from jax.experimental.pallas import tpu as pltpu
from jax.sharding import PartitionSpec as P

MESH = pl.DeviceIdType.MESH
BS = 256
ROWS = 4
HEAD = 16
NR = 8
NC = 16


class Streams:
    def __init__(self, send_sem, recv_sem):
        self.send_sem, self.recv_sem = send_sem, recv_sem
        self.number = {}
        self.started = []

    def copy(self, key, src, dst, device):
        at = self.number.setdefault(key, len(self.number))
        return pltpu.make_async_remote_copy(
            src_ref=src,
            dst_ref=dst,
            send_sem=self.send_sem.at[at],
            recv_sem=self.recv_sem.at[at],
            device_id=device,
            device_id_type=MESH,
        )

    def send(self, key, src, dst, device):
        copy = self.copy(key, src, dst, device)
        copy.start()
        self.started.append(copy)

    def arrived(self, key, dst, device):
        self.copy(key, dst, dst, device).wait_recv()


def kernel(
    values, columns, live, out, left, right, squared, ext, total, cube, send_sem, recv_sem
):
    row, col = lax.axis_index("row"), lax.axis_index("col")
    y_lo, z = row // 4, row % 4
    y_hi, x, core = col // 8, (col // 2) % 4, col % 2

    def row_of(dy, dz):
        return ((y_lo + dy) % 2) * 4 + (z + dz + 4) % 4

    def col_of(dy, dx, dc):
        return (((y_hi + dy) % 2) * 4 + (x + dx + 4) % 4) * 2 + (core + dc) % 2

    near = {
        "y": (row_of(1, 0), col),
        "z+": (row_of(0, 1), col),
        "z-": (row_of(0, -1), col),
        "x+": (row, col_of(0, 1, 0)),
        "x-": (row, col_of(0, -1, 0)),
        "h": (row, col_of(1, 0, 0)),
        "c": (row, col_of(0, 0, 1)),
    }
    barrier = pltpu.get_barrier_semaphore()
    for device in near.values():
        pl.semaphore_signal(barrier, inc=1, device_id=device, device_id_type=MESH)

    heads = [
        jnp.broadcast_to(columns[j, 0].astype(jnp.float32), (1, BS)) for j in range(ROWS)
    ]
    head = jnp.concatenate(
        heads + [jnp.zeros((HEAD - ROWS, BS), jnp.float32)], axis=0
    ).astype(jnp.bfloat16)
    left[col, 0:HEAD, :] = head
    right[row, 0:HEAD, :] = head
    for j in range(ROWS):
        block = (values[j, 0].astype(jnp.float32) * live[j, 0].astype(jnp.float32)).astype(
            jnp.bfloat16
        )
        left[col, HEAD + j * BS : HEAD + (j + 1) * BS, :] = block
        right[row, HEAD + j * BS : HEAD + (j + 1) * BS, :] = block
    pl.semaphore_wait(barrier, len(near))

    streams = Streams(send_sem, recv_sem)

    def piece(buffer, unit, j):
        if buffer is squared:
            return buffer.at[unit, pl.ds(j * BS, BS)]
        if j == 0:
            return buffer.at[unit, pl.ds(0, HEAD + BS)]
        return buffer.at[unit, pl.ds(HEAD + j * BS, BS)]

    def send(name, buffer, unit, j, way):
        ref = piece(buffer, unit, j)
        streams.send((name, j, way), ref, ref, near[way])

    def arrived(name, buffer, unit, j, way):
        streams.arrived((name, j, way), piece(buffer, unit, j), near[way])

    def right_own(tag, buffer, j):
        for way in ("y", "z+", "z-"):
            send(tag + "own", buffer, row, j, way)

    def right_ring(tag, buffer, j):
        arrived(tag + "own", buffer, row_of(0, -1), j, "z+")
        if j % 2 == 0:
            send(tag + "two", buffer, row_of(0, -1), j, "z+")
        arrived(tag + "own", buffer, row_of(0, 1), j, "z-")
        if j % 2 == 1:
            send(tag + "two", buffer, row_of(0, 1), j, "z-")

    def right_side(tag, buffer, j):
        arrived(tag + "own", buffer, row_of(1, 0), j, "y")
        send(tag + "side", buffer, row_of(1, 0), j, "z+")
        send(tag + "side", buffer, row_of(1, 0), j, "z-")

    def right_two(tag, buffer, j):
        arrived(tag + "two", buffer, row_of(0, 2), j, "z+" if j % 2 == 0 else "z-")
        send(tag + "far", buffer, row_of(0, 2), j, "y")

    def right_end(tag, buffer, j):
        arrived(tag + "side", buffer, row_of(1, -1), j, "z+")
        arrived(tag + "side", buffer, row_of(1, 1), j, "z-")
        arrived(tag + "far", buffer, row_of(1, 2), j, "y")

    def left_own(j):
        for way in ("h", "x+", "x-", "c"):
            send("Lown", left, col, j, way)

    def left_ring(j):
        arrived("Lown", left, col_of(0, -1, 0), j, "x+")
        if j % 2 == 0:
            send("Ltwo", left, col_of(0, -1, 0), j, "x+")
        send("Lm", left, col_of(0, -1, 0), j, "c")
        arrived("Lown", left, col_of(0, 1, 0), j, "x-")
        if j % 2 == 1:
            send("Ltwo", left, col_of(0, 1, 0), j, "x-")
        send("Lp", left, col_of(0, 1, 0), j, "c")

    def left_side(j):
        arrived("Lown", left, col_of(1, 0, 0), j, "h")
        for way in ("x+", "x-", "c"):
            send("Lside", left, col_of(1, 0, 0), j, way)

    def left_side_ring(j):
        arrived("Lside", left, col_of(1, -1, 0), j, "x+")
        if j % 2 == 1:
            send("Lfar", left, col_of(1, -1, 0), j, "x+")
        send("Lsm", left, col_of(1, -1, 0), j, "c")
        arrived("Lside", left, col_of(1, 1, 0), j, "x-")
        if j % 2 == 0:
            send("Lfar", left, col_of(1, 1, 0), j, "x-")
        send("Lsp", left, col_of(1, 1, 0), j, "c")

    def left_two(j):
        arrived("Ltwo", left, col_of(0, 2, 0), j, "x+" if j % 2 == 0 else "x-")
        send("Ltwo", left, col_of(0, 2, 0), j, "c")

    def left_far(j):
        arrived("Lfar", left, col_of(1, 2, 0), j, "x+" if j % 2 == 1 else "x-")
        send("Lfar", left, col_of(1, 2, 0), j, "c")

    def left_end(j):
        arrived("Lown", left, col_of(0, 0, 1), j, "c")
        arrived("Lm", left, col_of(0, -1, 1), j, "c")
        arrived("Lp", left, col_of(0, 1, 1), j, "c")
        arrived("Lside", left, col_of(1, 0, 1), j, "c")
        arrived("Lsm", left, col_of(1, -1, 1), j, "c")
        arrived("Lsp", left, col_of(1, 1, 1), j, "c")
        arrived("Ltwo", left, col_of(0, 2, 1), j, "c")
        arrived("Lfar", left, col_of(1, 2, 1), j, "c")

    def build_ext(i):
        mine = columns[i, 0].astype(jnp.float32)
        alive = (live[i, 0] > 0).astype(jnp.float32)

        def step(r, carry):
            right_head = right[r, 0:HEAD, :].astype(jnp.float32)
            for part in range(2):
                g = 2 * r + part
                own = left[g, 0:HEAD, :].astype(jnp.float32)[i : i + 1]
                block = left[g, HEAD + i * BS : HEAD + (i + 1) * BS, :]
                for b in range(2):
                    j = 2 * part + b
                    met = right_head[j : j + 1]
                    weight = jnp.where((own == float(b)) & (met == mine), alive, 0.0)
                    ext[r, i * BS : (i + 1) * BS, j * BS : (j + 1) * BS] = (
                        block * weight.astype(jnp.bfloat16)
                    )
            return carry

        lax.fori_loop(0, NR, step, 0)

    def square(i):
        total[...] = jnp.zeros_like(total)

        def step(r, carry):
            total[...] += jnp.dot(
                ext[r, i * BS : (i + 1) * BS, :],
                right[r, HEAD:, :],
                preferred_element_type=jnp.float32,
            )
            return carry

        lax.fori_loop(0, NR, step, 0)
        squared[row, i * BS : (i + 1) * BS, :] = total[...].astype(jnp.bfloat16)

    def cube_step(j):
        def step(r, carry):
            cube[...] += jnp.dot(
                ext[r, :, j * BS : (j + 1) * BS],
                squared[r, j * BS : (j + 1) * BS, :],
                preferred_element_type=jnp.float32,
            )
            return carry

        lax.fori_loop(0, NR, step, 0)

    every = range(ROWS)
    for j in every:
        right_own("R", right, j)
        left_own(j)
    cube[...] = jnp.zeros_like(cube)
    for j in every:
        right_ring("R", right, j)
        left_ring(j)
        right_side("R", right, j)
        left_side(j)
    for j in every:
        left_side_ring(j)
        left_two(j)
        right_two("R", right, j)
    for j in every:
        left_far(j)
    for j in every:
        right_end("R", right, j)
    for j in every:
        left_end(j)
        build_ext(j)
        square(j)
        right_own("S", squared, j)
        if j > 0:
            right_ring("S", squared, j - 1)
            right_side("S", squared, j - 1)
    right_ring("S", squared, 3)
    right_side("S", squared, 3)
    for j in every:
        right_two("S", squared, j)
    for j in every:
        right_end("S", squared, j)
        cube_step(j)
    for j in every:
        masked = left[col, HEAD + j * BS : HEAD + (j + 1) * BS, :].astype(jnp.float32)
        out[j, 0] = (1.5 * masked - 0.5 * cube[j * BS : (j + 1) * BS, :]).astype(jnp.bfloat16)
    for copy in streams.started:
        copy.wait_send()


COPIES = ROWS * (15 + 7 + 7)


def body(block_values, block_columns, block_live):
    return pl.pallas_call(
        kernel,
        name="sign_step",
        out_shape=jax.ShapeDtypeStruct(block_values.shape, jnp.bfloat16),
        in_specs=[
            pl.BlockSpec(memory_space=pltpu.VMEM),
            pl.BlockSpec(memory_space=pltpu.SMEM),
            pl.BlockSpec(memory_space=pltpu.SMEM),
        ],
        out_specs=pl.BlockSpec(memory_space=pltpu.VMEM),
        scratch_shapes=[
            pltpu.VMEM((NC, HEAD + ROWS * BS, BS), jnp.bfloat16),
            pltpu.VMEM((NR, HEAD + ROWS * BS, BS), jnp.bfloat16),
            pltpu.VMEM((NR, ROWS * BS, BS), jnp.bfloat16),
            pltpu.VMEM((NR, ROWS * BS, ROWS * BS), jnp.bfloat16),
            pltpu.VMEM((BS, BS), jnp.float32),
            pltpu.VMEM((ROWS * BS, BS), jnp.float32),
            pltpu.SemaphoreType.DMA((COPIES,)),
            pltpu.SemaphoreType.DMA((COPIES,)),
        ],
        compiler_params=pltpu.CompilerParams(
            collective_id=0, has_side_effects=True, vmem_limit_bytes=56 * 1024 * 1024
        ),
    )(block_values, block_columns, block_live)


def solution(mesh):
    return jax.shard_map(
        body,
        mesh=mesh,
        in_specs=(P("row", "col", None, None), P("row", "col"), P("row", "col")),
        out_specs=P("row", "col", None, None),
        check_vma=False,
    )
```

time: 386 us -> 93.6 us (0.24)
  waiting for transfers between devices: 229 us -> 0 us
  Pallas kernels: 0 us -> 89.5 us
  local copies, waits for them, and re-layouts: 68.7 us -> 3.87 us
  blocking collectives: 38.2 us -> 0 us
  matrix products: 22.5 us -> 0 us
  between operations: 14.2 us -> 0.01 us
  starting transfers between devices: 6.01 us -> 0 us
  other arithmetic: 5.42 us -> 0 us
    ppermute x21 -> x0, waiting for transfers between devices: 229 us -> none  [shifted(): lax.ppermute(value, axis, [(i, (i + by) % count) for i in range(count)])]
    pallas_call x0 -> x1, Pallas kernels: none -> 89.5 us  [body(): pl.pallas_call(kernel, name='sign_step', out_shape=jax.ShapeDtypeStruct(b...]
    gather x48 -> x0, local copies, waits for them, and re-layouts: 55.6 us -> none  [the longest x32 45.4 us: select_blocks(): chosen = jnp.take(right_values, position, axis=0)]
    psum x1 -> x0, blocking collectives: 38.2 us -> none  [from_root(): return lax.psum(block, axis)]
    dot_general x32 -> x0, matrix products: 22.5 us -> none  [multiply(): jnp.einsum('ijxy,ijyz->ixz', left_values, chosen, preferred_element_type=...]
    unnamed x100 -> x5, local copies, waits for them, and re-layouts: 13.1 us -> 3.87 us
    ppermute x21 -> x0, starting transfers between devices: 6 us -> none  [shifted(): lax.ppermute(value, axis, [(i, (i + by) % count) for i in range(count)])]
    another operation x2 -> x0, other arithmetic: 5.13 us -> none
  transfers between devices with their start and end apart: 22 -> 0, of which waited for: 16 -> 0; matrix products, arithmetic and copies ran while one was open for 12% -> 0% of each run, Pallas kernels for 0% -> 0%
where the time goes in v1:
time: 93.6 us; the launch traced here: 93.4 us
  Pallas kernels  89.5 us (96%)
  local copies, waits for them, and re-layouts  3.87 us (4%)
    pallas_call x1, Pallas kernels, body(): pl.pallas_call(kernel, name='sign_step', out_shape=jax.ShapeDtypeStruct(b...  89.5 us
    unnamed x5, local copies, waits for them, and re-layouts  3.87 us

profile of v1, /device:TPU:0, one launch (start us, length us, event | category | flops | bytes accessed | tf_op | source)
XLA Modules:
  0.0 93.4 jit_solution(16442110691166536977)
XLA Ops:
  0.0 0.0 copy-start
  0.0 1.3 %copy.4.columns = s32[4,1]{1,0:T(4,128)} copy(s32[4,1]{0,1:T(1,128)} %param.4) | data formatting | bytes 32 | tf_op args[1]
  1.3 0.0 copy-done
  1.3 0.7 copy.5.live
  2.0 89.5 %sign_step.1 = bf16[4,1,256,256]{3,2,1,0:T(8,128)(2,1)} custom-call(bf16[4,1,256,256]{3,2,1,0:T(8,128)(2,1)} %values.1, s32[4,1]{1,0:T(4,128)} %copy.4.columns, s32[4,1]{1,0:T(4,128)} %copy.5.live), custom_call_target="tpu_custom_call" | custom-call | tf_op jit(solution)/shard_map/sign_step/pallas_call | solution.py:265
  91.5 1.9 %copy.7 = bf16[4,1,256,256]{3,2,1,0:T(8,128)(2,1)} copy(bf16[4,1,256,256]{3,2,1,0:T(8,128)(2,1)} %sign_step.1) | data formatting | bytes 1048576
Async XLA Ops:
  0.0 1.3 %copy-start = (s32[4,1]{0,1:T(1,128)S(1)}, s32[4,1]{0,1:T(1,128)}, u32[]{:S(2)}) copy-start(s32[4,1]{0,1:T(1,128)} %param.5) | copy-start | bytes 52

commit v2 on v1

--- a/solution.py
+++ b/solution.py
@@ -42,7 +42,7 @@
 
 
 def kernel(
-    values, columns, live, out, left, right, squared, ext, total, cube, send_sem, recv_sem
+    values, columns, live, out, left, right, squared, chosen, cube, send_sem, recv_sem
 ):
     row, col = lax.axis_index("row"), lax.axis_index("col")
     y_lo, z = row // 4, row % 4
@@ -68,7 +68,7 @@
         pl.semaphore_signal(barrier, inc=1, device_id=device, device_id_type=MESH)
 
     heads = [
-        jnp.broadcast_to(columns[j, 0].astype(jnp.float32), (1, BS)) for j in range(ROWS)
+        jnp.broadcast_to(columns[0, j].astype(jnp.float32), (1, BS)) for j in range(ROWS)
     ]
     head = jnp.concatenate(
         heads + [jnp.zeros((HEAD - ROWS, BS), jnp.float32)], axis=0
@@ -76,7 +76,7 @@
     left[col, 0:HEAD, :] = head
     right[row, 0:HEAD, :] = head
     for j in range(ROWS):
-        block = (values[j, 0].astype(jnp.float32) * live[j, 0].astype(jnp.float32)).astype(
+        block = (values[j, 0].astype(jnp.float32) * live[0, j].astype(jnp.float32)).astype(
             jnp.bfloat16
         )
         left[col, HEAD + j * BS : HEAD + (j + 1) * BS, :] = block
@@ -126,8 +126,11 @@
         arrived(tag + "far", buffer, row_of(1, 2), j, "y")
 
     def left_own(j):
-        for way in ("h", "x+", "x-", "c"):
+        for way in ("x+", "x-", "c"):
             send("Lown", left, col, j, way)
+
+    def left_hop(j):
+        send("Lown", left, col, j, "h")
 
     def left_ring(j):
         arrived("Lown", left, col_of(0, -1, 0), j, "x+")
@@ -172,57 +175,60 @@
         arrived("Ltwo", left, col_of(0, 2, 1), j, "c")
         arrived("Lfar", left, col_of(1, 2, 1), j, "c")
 
-    def build_ext(i):
-        mine = columns[i, 0].astype(jnp.float32)
-        alive = (live[i, 0] > 0).astype(jnp.float32)
-
-        def step(r, carry):
+    def select(buffer, first, i, parts):
+        mine = columns[0, i].astype(jnp.float32)
+        alive = (live[0, i] > 0).astype(jnp.float32)
+        for r in range(NR):
             right_head = right[r, 0:HEAD, :].astype(jnp.float32)
-            for part in range(2):
+            for part in parts:
                 g = 2 * r + part
                 own = left[g, 0:HEAD, :].astype(jnp.float32)[i : i + 1]
-                block = left[g, HEAD + i * BS : HEAD + (i + 1) * BS, :]
+                weights = []
                 for b in range(2):
-                    j = 2 * part + b
-                    met = right_head[j : j + 1]
-                    weight = jnp.where((own == float(b)) & (met == mine), alive, 0.0)
-                    ext[r, i * BS : (i + 1) * BS, j * BS : (j + 1) * BS] = (
-                        block * weight.astype(jnp.bfloat16)
+                    met = right_head[2 * part + b : 2 * part + b + 1]
+                    weights.append(
+                        jnp.where((own == float(b)) & (met == mine), alive, 0.0).astype(
+                            jnp.bfloat16
+                        )
                     )
-            return carry
-
-        lax.fori_loop(0, NR, step, 0)
+                at = first + 2 * part * BS
+                chosen[g * BS : (g + 1) * BS, :] = (
+                    buffer[r, at : at + BS, :] * weights[0]
+                    + buffer[r, at + BS : at + 2 * BS, :] * weights[1]
+                )
+
+    def product(i, parts):
+        groups = [2 * r + part for r in range(NR) for part in parts]
+        rows = jnp.concatenate(
+            [left[g, HEAD + i * BS : HEAD + (i + 1) * BS, :] for g in groups], axis=1
+        )
+        return jnp.dot(
+            rows,
+            jnp.concatenate([chosen[g * BS : (g + 1) * BS, :] for g in groups], axis=0),
+            preferred_element_type=jnp.float32,
+        )
 
     def square(i):
-        total[...] = jnp.zeros_like(total)
-
-        def step(r, carry):
-            total[...] += jnp.dot(
-                ext[r, i * BS : (i + 1) * BS, :],
-                right[r, HEAD:, :],
-                preferred_element_type=jnp.float32,
-            )
-            return carry
-
-        lax.fori_loop(0, NR, step, 0)
-        squared[row, i * BS : (i + 1) * BS, :] = total[...].astype(jnp.bfloat16)
-
-    def cube_step(j):
-        def step(r, carry):
-            cube[...] += jnp.dot(
-                ext[r, :, j * BS : (j + 1) * BS],
-                squared[r, j * BS : (j + 1) * BS, :],
-                preferred_element_type=jnp.float32,
-            )
-            return carry
-
-        lax.fori_loop(0, NR, step, 0)
+        select(right, HEAD, i, (0, 1))
+        squared[row, i * BS : (i + 1) * BS, :] = product(i, (0, 1)).astype(jnp.bfloat16)
+
+    def cube_even():
+        for i in range(ROWS):
+            select(squared, 0, i, (0,))
+            cube[i * BS : (i + 1) * BS, :] = product(i, (0,))
+
+    def finish():
+        for i in range(ROWS):
+            select(squared, 0, i, (1,))
+            cube_part = cube[i * BS : (i + 1) * BS, :] + product(i, (1,))
+            masked = left[col, HEAD + i * BS : HEAD + (i + 1) * BS, :].astype(jnp.float32)
+            out[i, 0] = (1.5 * masked - 0.5 * cube_part).astype(jnp.bfloat16)
 
     every = range(ROWS)
     for j in every:
         right_own("R", right, j)
         left_own(j)
-    cube[...] = jnp.zeros_like(cube)
+        left_hop(j)
     for j in every:
         right_ring("R", right, j)
         left_ring(j)
@@ -238,7 +244,6 @@
         right_end("R", right, j)
     for j in every:
         left_end(j)
-        build_ext(j)
         square(j)
         right_own("S", squared, j)
         if j > 0:
@@ -248,12 +253,12 @@
     right_side("S", squared, 3)
     for j in every:
         right_two("S", squared, j)
-    for j in every:
+    for j in (0, 1):
         right_end("S", squared, j)
-        cube_step(j)
-    for j in every:
-        masked = left[col, HEAD + j * BS : HEAD + (j + 1) * BS, :].astype(jnp.float32)
-        out[j, 0] = (1.5 * masked - 0.5 * cube[j * BS : (j + 1) * BS, :]).astype(jnp.bfloat16)
+    cube_even()
+    for j in (2, 3):
+        right_end("S", squared, j)
+    finish()
     for copy in streams.started:
         copy.wait_send()
 
@@ -276,8 +281,7 @@
             pltpu.VMEM((NC, HEAD + ROWS * BS, BS), jnp.bfloat16),
             pltpu.VMEM((NR, HEAD + ROWS * BS, BS), jnp.bfloat16),
             pltpu.VMEM((NR, ROWS * BS, BS), jnp.bfloat16),
-            pltpu.VMEM((NR, ROWS * BS, ROWS * BS), jnp.bfloat16),
-            pltpu.VMEM((BS, BS), jnp.float32),
+            pltpu.VMEM((NC * BS, BS), jnp.bfloat16),
             pltpu.VMEM((ROWS * BS, BS), jnp.float32),
             pltpu.SemaphoreType.DMA((COPIES,)),
             pltpu.SemaphoreType.DMA((COPIES,)),
@@ -285,7 +289,7 @@
         compiler_params=pltpu.CompilerParams(
             collective_id=0, has_side_effects=True, vmem_limit_bytes=56 * 1024 * 1024
         ),
-    )(block_values, block_columns, block_live)
+    )(block_values, block_columns.T, block_live.T)
 
 
 def solution(mesh):

time: 93.6 us -> 84 us (0.90)
  Pallas kernels: 89.5 us -> 81.9 us
  local copies, waits for them, and re-layouts: 3.87 us -> 1.87 us
    pallas_call x1, Pallas kernels: 89.5 us -> 81.9 us  [body(): pl.pallas_call(kernel, name='sign_step', out_shape=jax.ShapeDtypeStruct(b...]
    unnamed x5 -> x1, local copies, waits for them, and re-layouts: 3.87 us -> 1.87 us
where the time goes in v2:
time: 84 us; the launch traced here: 83.8 us
  Pallas kernels  81.9 us (98%)
  local copies, waits for them, and re-layouts  1.87 us (2%)
    pallas_call x1, Pallas kernels, body(): pl.pallas_call(kernel, name='sign_step', out_shape=jax.ShapeDtypeStruct(b...  81.9 us
    unnamed x1, local copies, waits for them, and re-layouts  1.87 us

profile of v2, /device:TPU:0, one launch (start us, length us, event | category | flops | bytes accessed | tf_op | source)
XLA Modules:
  0.0 83.8 jit_solution(15166592934879336295)
XLA Ops:
  0.0 81.9 %sign_step.1 = bf16[4,1,256,256]{3,2,1,0:T(8,128)(2,1)} custom-call(bf16[4,1,256,256]{3,2,1,0:T(8,128)(2,1)} %values.1, s32[1,4]{1,0:T(1,128)} %bitcast.2, s32[1,4]{1,0:T(1,128)} %bitcast.3), custom_call_target="tpu_custom_call" | custom-call | tf_op jit(solution)/shard_map/sign_step/pallas_call | solution.py:270
  81.9 1.9 %copy.5 = bf16[4,1,256,256]{3,2,1,0:T(8,128)(2,1)} copy(bf16[4,1,256,256]{3,2,1,0:T(8,128)(2,1)} %sign_step.1) | data formatting | bytes 1048576

commit v3 on v2

--- a/solution.py
+++ b/solution.py
@@ -13,6 +13,133 @@
 HEAD = 16
 NR = 8
 NC = 16
+
+
+PATHS = {
+    ("R", "two"): "++--",
+    ("R", "far"): "++yy",
+    ("R", "m"): "zzzy",
+    ("R", "p"): "zzzz",
+    ("S", "two"): "--++",
+    ("S", "far"): "y-y+",
+    ("S", "m"): "yzyz",
+    ("S", "p"): "yzyz",
+    ("L", "two"): "-+-+",
+    ("L", "far"): "--++",
+}
+
+ORDER = (
+    ("R", "own", 0),
+    ("R", "own", 1),
+    ("R", "own", 3),
+    ("L", "own", 0),
+    ("L", "own", 1),
+    ("L", "p", 0),
+    ("L", "hop", 1),
+    ("L", "own", 3),
+    ("L", "hop", 0),
+    ("R", "side", 1),
+    ("L", "own", 2),
+    ("R", "own", 2),
+    ("R", "side", 0),
+    ("L", "m", 1),
+    ("R", "m", 1),
+    ("L", "m", 3),
+    ("R", "p", 3),
+    ("L", "hop", 3),
+    ("L", "hop", 2),
+    ("L", "p", 3),
+    ("L", "side", 1),
+    ("R", "p", 0),
+    ("R", "m", 3),
+    ("L", "m", 0),
+    ("R", "p", 1),
+    ("R", "m", 0),
+    ("R", "p", 2),
+    ("L", "side", 0),
+    ("L", "sp", 1),
+    ("R", "side", 3),
+    ("R", "side", 2),
+    ("L", "sp", 0),
+    ("R", "two", 3),
+    ("L", "side", 3),
+    ("R", "sideM", 1),
+    ("L", "sm", 0),
+    ("R", "two", 1),
+    ("L", "p", 2),
+    ("R", "sideM", 0),
+    ("R", "sideP", 1),
+    ("R", "two", 2),
+    ("L", "two", 3),
+    ("L", "side", 2),
+    ("L", "two", 1),
+    ("L", "p", 1),
+    ("L", "far", 1),
+    ("R", "two", 0),
+    ("R", "sideP", 3),
+    ("R", "m", 2),
+    ("L", "far", 0),
+    ("L", "sm", 3),
+    ("L", "sm", 1),
+    ("L", "two", 0),
+    ("R", "sideM", 3),
+    ("L", "sp", 3),
+    ("R", "sideM", 2),
+    ("L", "end", 0),
+    ("R", "sideP", 2),
+    ("L", "sm", 2),
+    ("R", "far", 3),
+    ("R", "far", 1),
+    ("L", "end", 1),
+    ("L", "m", 2),
+    ("R", "sideP", 0),
+    ("R", "far", 2),
+    ("R", "far", 0),
+    ("C", "square", 0),
+    ("S", "own", 0),
+    ("C", "square", 1),
+    ("S", "own", 1),
+    ("L", "far", 3),
+    ("L", "far", 2),
+    ("L", "end", 3),
+    ("C", "square", 3),
+    ("L", "two", 2),
+    ("S", "own", 3),
+    ("L", "sp", 2),
+    ("S", "m", 0),
+    ("S", "p", 0),
+    ("L", "end", 2),
+    ("C", "square", 2),
+    ("S", "m", 1),
+    ("S", "own", 2),
+    ("S", "side", 1),
+    ("S", "side", 3),
+    ("S", "m", 2),
+    ("S", "p", 1),
+    ("S", "p", 2),
+    ("S", "sideP", 1),
+    ("S", "m", 3),
+    ("S", "two", 0),
+    ("S", "sideM", 3),
+    ("S", "sideP", 3),
+    ("S", "two", 2),
+    ("S", "far", 1),
+    ("S", "sideM", 0),
+    ("S", "p", 3),
+    ("S", "side", 0),
+    ("S", "far", 3),
+    ("S", "sideP", 0),
+    ("S", "sideP", 2),
+    ("S", "two", 3),
+    ("S", "far", 0),
+    ("S", "sideM", 2),
+    ("S", "side", 2),
+    ("S", "two", 1),
+    ("S", "sideM", 1),
+    ("C", "even", 0),
+    ("S", "far", 2),
+    ("C", "finish", 0),
+)
 
 
 class Streams:
@@ -99,81 +226,90 @@
     def arrived(name, buffer, unit, j, way):
         streams.arrived((name, j, way), piece(buffer, unit, j), near[way])
 
-    def right_own(tag, buffer, j):
-        for way in ("y", "z+", "z-"):
-            send(tag + "own", buffer, row, j, way)
-
-    def right_ring(tag, buffer, j):
-        arrived(tag + "own", buffer, row_of(0, -1), j, "z+")
-        if j % 2 == 0:
-            send(tag + "two", buffer, row_of(0, -1), j, "z+")
-        arrived(tag + "own", buffer, row_of(0, 1), j, "z-")
-        if j % 2 == 1:
-            send(tag + "two", buffer, row_of(0, 1), j, "z-")
-
-    def right_side(tag, buffer, j):
-        arrived(tag + "own", buffer, row_of(1, 0), j, "y")
-        send(tag + "side", buffer, row_of(1, 0), j, "z+")
-        send(tag + "side", buffer, row_of(1, 0), j, "z-")
-
-    def right_two(tag, buffer, j):
-        arrived(tag + "two", buffer, row_of(0, 2), j, "z+" if j % 2 == 0 else "z-")
-        send(tag + "far", buffer, row_of(0, 2), j, "y")
-
-    def right_end(tag, buffer, j):
-        arrived(tag + "side", buffer, row_of(1, -1), j, "z+")
-        arrived(tag + "side", buffer, row_of(1, 1), j, "z-")
-        arrived(tag + "far", buffer, row_of(1, 2), j, "y")
-
-    def left_own(j):
-        for way in ("x+", "x-", "c"):
-            send("Lown", left, col, j, way)
-
-    def left_hop(j):
-        send("Lown", left, col, j, "h")
-
-    def left_ring(j):
-        arrived("Lown", left, col_of(0, -1, 0), j, "x+")
-        if j % 2 == 0:
-            send("Ltwo", left, col_of(0, -1, 0), j, "x+")
-        send("Lm", left, col_of(0, -1, 0), j, "c")
-        arrived("Lown", left, col_of(0, 1, 0), j, "x-")
-        if j % 2 == 1:
-            send("Ltwo", left, col_of(0, 1, 0), j, "x-")
-        send("Lp", left, col_of(0, 1, 0), j, "c")
-
-    def left_side(j):
-        arrived("Lown", left, col_of(1, 0, 0), j, "h")
-        for way in ("x+", "x-", "c"):
-            send("Lside", left, col_of(1, 0, 0), j, way)
-
-    def left_side_ring(j):
-        arrived("Lside", left, col_of(1, -1, 0), j, "x+")
-        if j % 2 == 1:
-            send("Lfar", left, col_of(1, -1, 0), j, "x+")
-        send("Lsm", left, col_of(1, -1, 0), j, "c")
-        arrived("Lside", left, col_of(1, 1, 0), j, "x-")
-        if j % 2 == 0:
-            send("Lfar", left, col_of(1, 1, 0), j, "x-")
-        send("Lsp", left, col_of(1, 1, 0), j, "c")
-
-    def left_two(j):
-        arrived("Ltwo", left, col_of(0, 2, 0), j, "x+" if j % 2 == 0 else "x-")
-        send("Ltwo", left, col_of(0, 2, 0), j, "c")
-
-    def left_far(j):
-        arrived("Lfar", left, col_of(1, 2, 0), j, "x+" if j % 2 == 1 else "x-")
-        send("Lfar", left, col_of(1, 2, 0), j, "c")
-
-    def left_end(j):
-        arrived("Lown", left, col_of(0, 0, 1), j, "c")
-        arrived("Lm", left, col_of(0, -1, 1), j, "c")
-        arrived("Lp", left, col_of(0, 1, 1), j, "c")
-        arrived("Lside", left, col_of(1, 0, 1), j, "c")
-        arrived("Lsm", left, col_of(1, -1, 1), j, "c")
-        arrived("Lsp", left, col_of(1, 1, 1), j, "c")
-        arrived("Ltwo", left, col_of(0, 2, 1), j, "c")
-        arrived("Lfar", left, col_of(1, 2, 1), j, "c")
+    def right_step(tag, buffer, name, j):
+        two, far, side_m, side_p = (PATHS[tag, k][j] for k in ("two", "far", "m", "p"))
+        if name == "own":
+            for way in ("y", "z+", "z-"):
+                send(tag + "own", buffer, row, j, way)
+        elif name == "m":
+            arrived(tag + "own", buffer, row_of(0, -1), j, "z+")
+            if two == "+":
+                send(tag + "two", buffer, row_of(0, -1), j, "z+")
+            if side_m == "y":
+                send(tag + "sideM", buffer, row_of(0, -1), j, "y")
+        elif name == "p":
+            arrived(tag + "own", buffer, row_of(0, 1), j, "z-")
+            if two == "-":
+                send(tag + "two", buffer, row_of(0, 1), j, "z-")
+            if side_p == "y":
+                send(tag + "sideP", buffer, row_of(0, 1), j, "y")
+        elif name == "side":
+            arrived(tag + "own", buffer, row_of(1, 0), j, "y")
+            if side_m == "z":
+                send(tag + "sideM", buffer, row_of(1, 0), j, "z+")
+            if side_p == "z":
+                send(tag + "sideP", buffer, row_of(1, 0), j, "z-")
+        elif name == "two":
+            arrived(tag + "two", buffer, row_of(0, 2), j, "z" + two)
+            if far == "y":
+                send(tag + "far", buffer, row_of(0, 2), j, "y")
+        elif name == "sideM":
+            arrived(tag + "sideM", buffer, row_of(1, -1), j, "z+" if side_m == "z" else "y")
+            if far == "+":
+                send(tag + "far", buffer, row_of(1, -1), j, "z+")
+        elif name == "sideP":
+            arrived(tag + "sideP", buffer, row_of(1, 1), j, "z-" if side_p == "z" else "y")
+            if far == "-":
+                send(tag + "far", buffer, row_of(1, 1), j, "z-")
+        elif name == "far":
+            arrived(tag + "far", buffer, row_of(1, 2), j, "y" if far == "y" else "z" + far)
+
+    def left_step(name, j):
+        two, far = (PATHS["L", k][j] for k in ("two", "far"))
+        if name == "own":
+            for way in ("x+", "x-", "c"):
+                send("Lown", left, col, j, way)
+        elif name == "hop":
+            send("Lown", left, col, j, "h")
+        elif name == "m":
+            arrived("Lown", left, col_of(0, -1, 0), j, "x+")
+            if two == "+":
+                send("Ltwo", left, col_of(0, -1, 0), j, "x+")
+            send("Lm", left, col_of(0, -1, 0), j, "c")
+        elif name == "p":
+            arrived("Lown", left, col_of(0, 1, 0), j, "x-")
+            if two == "-":
+                send("Ltwo", left, col_of(0, 1, 0), j, "x-")
+            send("Lp", left, col_of(0, 1, 0), j, "c")
+        elif name == "side":
+            arrived("Lown", left, col_of(1, 0, 0), j, "h")
+            for way in ("x+", "x-", "c"):
+                send("Lside", left, col_of(1, 0, 0), j, way)
+        elif name == "sm":
+            arrived("Lside", left, col_of(1, -1, 0), j, "x+")
+            if far == "+":
+                send("Lfar", left, col_of(1, -1, 0), j, "x+")
+            send("Lsm", left, col_of(1, -1, 0), j, "c")
+        elif name == "sp":
+            arrived("Lside", left, col_of(1, 1, 0), j, "x-")
+            if far == "-":
+                send("Lfar", left, col_of(1, 1, 0), j, "x-")
+            send("Lsp", left, col_of(1, 1, 0), j, "c")
+        elif name == "two":
+            arrived("Ltwo", left, col_of(0, 2, 0), j, "x" + two)
+            send("Ltwo", left, col_of(0, 2, 0), j, "c")
+        elif name == "far":
+            arrived("Lfar", left, col_of(1, 2, 0), j, "x" + far)
+            send("Lfar", left, col_of(1, 2, 0), j, "c")
+        elif name == "end":
+            arrived("Lown", left, col_of(0, 0, 1), j, "c")
+            arrived("Lm", left, col_of(0, -1, 1), j, "c")
+            arrived("Lp", left, col_of(0, 1, 1), j, "c")
+            arrived("Lside", left, col_of(1, 0, 1), j, "c")
+            arrived("Lsm", left, col_of(1, -1, 1), j, "c")
+            arrived("Lsp", left, col_of(1, 1, 1), j, "c")
+            arrived("Ltwo", left, col_of(0, 2, 1), j, "c")
+            arrived("Lfar", left, col_of(1, 2, 1), j, "c")
 
     def select(buffer, first, i, parts):
         mine = columns[0, i].astype(jnp.float32)
@@ -224,41 +360,19 @@
             masked = left[col, HEAD + i * BS : HEAD + (i + 1) * BS, :].astype(jnp.float32)
             out[i, 0] = (1.5 * masked - 0.5 * cube_part).astype(jnp.bfloat16)
 
-    every = range(ROWS)
-    for j in every:
-        right_own("R", right, j)
-        left_own(j)
-        left_hop(j)
-    for j in every:
-        right_ring("R", right, j)
-        left_ring(j)
-        right_side("R", right, j)
-        left_side(j)
-    for j in every:
-        left_side_ring(j)
-        left_two(j)
-        right_two("R", right, j)
-    for j in every:
-        left_far(j)
-    for j in every:
-        right_end("R", right, j)
-    for j in every:
-        left_end(j)
-        square(j)
-        right_own("S", squared, j)
-        if j > 0:
-            right_ring("S", squared, j - 1)
-            right_side("S", squared, j - 1)
-    right_ring("S", squared, 3)
-    right_side("S", squared, 3)
-    for j in every:
-        right_two("S", squared, j)
-    for j in (0, 1):
-        right_end("S", squared, j)
-    cube_even()
-    for j in (2, 3):
-        right_end("S", squared, j)
-    finish()
+    for tag, name, j in ORDER:
+        if tag == "R":
+            right_step(tag, right, name, j)
+        elif tag == "S":
+            right_step(tag, squared, name, j)
+        elif tag == "L":
+            left_step(name, j)
+        elif name == "square":
+            square(j)
+        elif name == "even":
+            cube_even()
+        else:
+            finish()
     for copy in streams.started:
         copy.wait_send()
 

time: 84 us -> 77.5 us (0.923)
  Pallas kernels: 81.9 us -> 75.1 us
    pallas_call x1, Pallas kernels: 81.9 us -> 75.1 us  [body(): pl.pallas_call(kernel, name='sign_step', out_shape=jax.ShapeDtypeStruct(b...]
where the time goes in v3:
time: 77.5 us; the launch traced here: 77 us
  Pallas kernels  75.1 us (97%)
  local copies, waits for them, and re-layouts  1.87 us (2%)
    pallas_call x1, Pallas kernels, body(): pl.pallas_call(kernel, name='sign_step', out_shape=jax.ShapeDtypeStruct(b...  75.1 us
    unnamed x1, local copies, waits for them, and re-layouts  1.87 us

profile of v3, /device:TPU:0, one launch (start us, length us, event | category | flops | bytes accessed | tf_op | source)
XLA Modules:
  0.0 77.0 jit_solution(10476293836648070128)
XLA Ops:
  0.0 75.1 %sign_step.1 = bf16[4,1,256,256]{3,2,1,0:T(8,128)(2,1)} custom-call(bf16[4,1,256,256]{3,2,1,0:T(8,128)(2,1)} %values.1, s32[1,4]{1,0:T(1,128)} %bitcast.2, s32[1,4]{1,0:T(1,128)} %bitcast.3), custom_call_target="tpu_custom_call" | custom-call | tf_op jit(solution)/shard_map/sign_step/pallas_call | solution.py:384
  75.1 1.9 %copy.5 = bf16[4,1,256,256]{3,2,1,0:T(8,128)(2,1)} copy(bf16[4,1,256,256]{3,2,1,0:T(8,128)(2,1)} %sign_step.1) | data formatting | bytes 1048576

commit v4 on v3

--- a/solution.py
+++ b/solution.py
@@ -11,133 +11,135 @@
 BS = 256
 ROWS = 4
 HEAD = 16
+PIECES = 4
+PIECE = ROWS * BS // PIECES
 NR = 8
 NC = 16
 
 
 PATHS = {
-    ("R", "two"): "++--",
-    ("R", "far"): "++yy",
-    ("R", "m"): "zzzy",
-    ("R", "p"): "zzzz",
-    ("S", "two"): "--++",
-    ("S", "far"): "y-y+",
-    ("S", "m"): "yzyz",
-    ("S", "p"): "yzyz",
+    ("R", "two"): "--++",
+    ("R", "far"): "+-y-",
+    ("R", "m"): "zzzz",
+    ("R", "p"): "yzyz",
+    ("S", "two"): "-+-+",
+    ("S", "far"): "y+y-",
+    ("S", "m"): "zyzz",
+    ("S", "p"): "yzzy",
     ("L", "two"): "-+-+",
-    ("L", "far"): "--++",
+    ("L", "far"): "+-+-",
 }
 
 ORDER = (
+    ("R", "own", 3),
+    ("R", "own", 1),
+    ("L", "hop", 1),
+    ("L", "hop", 0),
     ("R", "own", 0),
-    ("R", "own", 1),
-    ("R", "own", 3),
+    ("L", "own", 3),
+    ("R", "own", 2),
     ("L", "own", 0),
+    ("L", "own", 2),
+    ("L", "hop", 3),
+    ("R", "side", 1),
+    ("R", "side", 3),
+    ("L", "hop", 2),
+    ("L", "m", 3),
+    ("L", "p", 0),
     ("L", "own", 1),
-    ("L", "p", 0),
-    ("L", "hop", 1),
-    ("L", "own", 3),
-    ("L", "hop", 0),
-    ("R", "side", 1),
-    ("L", "own", 2),
-    ("R", "own", 2),
+    ("L", "side", 1),
+    ("L", "two", 0),
+    ("L", "m", 2),
+    ("L", "side", 0),
+    ("R", "m", 2),
+    ("R", "m", 1),
     ("R", "side", 0),
+    ("R", "p", 0),
     ("L", "m", 1),
-    ("R", "m", 1),
-    ("L", "m", 3),
-    ("R", "p", 3),
-    ("L", "hop", 3),
-    ("L", "hop", 2),
-    ("L", "p", 3),
-    ("L", "side", 1),
-    ("R", "p", 0),
+    ("R", "p", 1),
     ("R", "m", 3),
-    ("L", "m", 0),
-    ("R", "p", 1),
-    ("R", "m", 0),
-    ("R", "p", 2),
-    ("L", "side", 0),
+    ("R", "side", 2),
     ("L", "sp", 1),
-    ("R", "side", 3),
-    ("R", "side", 2),
-    ("L", "sp", 0),
-    ("R", "two", 3),
-    ("L", "side", 3),
-    ("R", "sideM", 1),
-    ("L", "sm", 0),
-    ("R", "two", 1),
-    ("L", "p", 2),
-    ("R", "sideM", 0),
     ("R", "sideP", 1),
     ("R", "two", 2),
+    ("L", "sm", 0),
+    ("R", "sideM", 1),
+    ("L", "m", 0),
+    ("L", "side", 3),
+    ("L", "p", 1),
+    ("R", "p", 2),
+    ("R", "sideP", 3),
+    ("R", "two", 0),
     ("L", "two", 3),
+    ("L", "two", 1),
     ("L", "side", 2),
-    ("L", "two", 1),
-    ("L", "p", 1),
+    ("L", "sm", 1),
+    ("R", "two", 1),
+    ("R", "sideM", 0),
+    ("L", "p", 3),
+    ("R", "two", 3),
     ("L", "far", 1),
-    ("R", "two", 0),
-    ("R", "sideP", 3),
-    ("R", "m", 2),
+    ("L", "sp", 3),
+    ("R", "p", 3),
+    ("L", "end", 1),
     ("L", "far", 0),
+    ("R", "sideM", 3),
+    ("L", "sp", 0),
+    ("R", "sideM", 2),
+    ("L", "sp", 2),
+    ("R", "m", 0),
+    ("R", "far", 1),
+    ("L", "end", 0),
+    ("R", "far", 3),
+    ("L", "p", 2),
+    ("R", "far", 2),
+    ("R", "sideP", 0),
     ("L", "sm", 3),
-    ("L", "sm", 1),
-    ("L", "two", 0),
-    ("R", "sideM", 3),
-    ("L", "sp", 3),
-    ("R", "sideM", 2),
-    ("L", "end", 0),
+    ("R", "far", 0),
     ("R", "sideP", 2),
-    ("L", "sm", 2),
-    ("R", "far", 3),
-    ("R", "far", 1),
-    ("L", "end", 1),
-    ("L", "m", 2),
-    ("R", "sideP", 0),
-    ("R", "far", 2),
-    ("R", "far", 0),
     ("C", "square", 0),
     ("S", "own", 0),
     ("C", "square", 1),
+    ("L", "far", 3),
+    ("L", "sm", 2),
     ("S", "own", 1),
-    ("L", "far", 3),
-    ("L", "far", 2),
     ("L", "end", 3),
     ("C", "square", 3),
+    ("S", "own", 3),
+    ("L", "far", 2),
+    ("S", "p", 0),
+    ("S", "side", 0),
     ("L", "two", 2),
-    ("S", "own", 3),
-    ("L", "sp", 2),
-    ("S", "m", 0),
-    ("S", "p", 0),
     ("L", "end", 2),
     ("C", "square", 2),
     ("S", "m", 1),
     ("S", "own", 2),
     ("S", "side", 1),
+    ("S", "sideP", 0),
     ("S", "side", 3),
+    ("S", "m", 0),
+    ("S", "p", 2),
+    ("S", "p", 3),
+    ("S", "two", 0),
+    ("S", "sideM", 1),
+    ("S", "side", 2),
+    ("S", "two", 2),
+    ("S", "m", 3),
+    ("S", "sideP", 3),
+    ("S", "far", 1),
+    ("S", "p", 1),
     ("S", "m", 2),
-    ("S", "p", 1),
-    ("S", "p", 2),
+    ("S", "two", 1),
     ("S", "sideP", 1),
-    ("S", "m", 3),
-    ("S", "two", 0),
+    ("S", "sideM", 2),
+    ("S", "sideM", 0),
     ("S", "sideM", 3),
-    ("S", "sideP", 3),
-    ("S", "two", 2),
-    ("S", "far", 1),
-    ("S", "sideM", 0),
-    ("S", "p", 3),
-    ("S", "side", 0),
-    ("S", "far", 3),
-    ("S", "sideP", 0),
-    ("S", "sideP", 2),
-    ("S", "two", 3),
     ("S", "far", 0),
-    ("S", "sideM", 2),
-    ("S", "side", 2),
-    ("S", "two", 1),
-    ("S", "sideM", 1),
     ("C", "even", 0),
     ("S", "far", 2),
+    ("S", "sideP", 2),
+    ("S", "far", 3),
+    ("S", "two", 3),
     ("C", "finish", 0),
 )
 
@@ -169,7 +171,7 @@
 
 
 def kernel(
-    values, columns, live, out, left, right, squared, chosen, cube, send_sem, recv_sem
+    values_in, columns_in, live_in, out, values, columns, live, left, right, squared, chosen, cube, in_sem, send_sem, recv_sem
 ):
     row, col = lax.axis_index("row"), lax.axis_index("col")
     y_lo, z = row // 4, row % 4
@@ -193,6 +195,17 @@
     barrier = pltpu.get_barrier_semaphore()
     for device in near.values():
         pl.semaphore_signal(barrier, inc=1, device_id=device, device_id_type=MESH)
+
+    fetches = [
+        pltpu.make_async_copy(source, target, in_sem.at[at])
+        for at, (source, target) in enumerate(
+            ((columns_in, columns), (live_in, live), (values_in, values))
+        )
+    ]
+    for fetch in fetches:
+        fetch.start()
+    for fetch in fetches:
+        fetch.wait()
 
     heads = [
         jnp.broadcast_to(columns[0, j].astype(jnp.float32), (1, BS)) for j in range(ROWS)
@@ -214,10 +227,10 @@
 
     def piece(buffer, unit, j):
         if buffer is squared:
-            return buffer.at[unit, pl.ds(j * BS, BS)]
+            return buffer.at[unit, pl.ds(j * PIECE, PIECE)]
         if j == 0:
-            return buffer.at[unit, pl.ds(0, HEAD + BS)]
-        return buffer.at[unit, pl.ds(HEAD + j * BS, BS)]
+            return buffer.at[unit, pl.ds(0, HEAD + PIECE)]
+        return buffer.at[unit, pl.ds(HEAD + j * PIECE, PIECE)]
 
     def send(name, buffer, unit, j, way):
         ref = piece(buffer, unit, j)
@@ -377,7 +390,7 @@
         copy.wait_send()
 
 
-COPIES = ROWS * (15 + 7 + 7)
+COPIES = PIECES * (15 + 7 + 7)
 
 
 def body(block_values, block_columns, block_live):
@@ -386,22 +399,26 @@
         name="sign_step",
         out_shape=jax.ShapeDtypeStruct(block_values.shape, jnp.bfloat16),
         in_specs=[
-            pl.BlockSpec(memory_space=pltpu.VMEM),
-            pl.BlockSpec(memory_space=pltpu.SMEM),
-            pl.BlockSpec(memory_space=pltpu.SMEM),
+            pl.BlockSpec(memory_space=pltpu.HBM),
+            pl.BlockSpec(memory_space=pltpu.HBM),
+            pl.BlockSpec(memory_space=pltpu.HBM),
         ],
         out_specs=pl.BlockSpec(memory_space=pltpu.VMEM),
         scratch_shapes=[
+            pltpu.VMEM(block_values.shape, jnp.bfloat16),
+            pltpu.SMEM((1, ROWS), jnp.int32),
+            pltpu.SMEM((1, ROWS), jnp.int32),
             pltpu.VMEM((NC, HEAD + ROWS * BS, BS), jnp.bfloat16),
             pltpu.VMEM((NR, HEAD + ROWS * BS, BS), jnp.bfloat16),
             pltpu.VMEM((NR, ROWS * BS, BS), jnp.bfloat16),
             pltpu.VMEM((NC * BS, BS), jnp.bfloat16),
             pltpu.VMEM((ROWS * BS, BS), jnp.float32),
+            pltpu.SemaphoreType.DMA((3,)),
             pltpu.SemaphoreType.DMA((COPIES,)),
             pltpu.SemaphoreType.DMA((COPIES,)),
         ],
         compiler_params=pltpu.CompilerParams(
-            collective_id=0, has_side_effects=True, vmem_limit_bytes=56 * 1024 * 1024
+            collective_id=0, has_side_effects=True, vmem_limit_bytes=28 * 1024 * 1024
         ),
     )(block_values, block_columns.T, block_live.T)
 

time: 77.5 us -> 76.1 us (0.982)
  Pallas kernels: 75.1 us -> 73 us
    pallas_call x1, Pallas kernels: 75.1 us -> 73 us  [body(): pl.pallas_call(kernel, name='sign_step', out_shape=jax.ShapeDtypeStruct(b...]
    unnamed x1 -> x7, local copies, waits for them, and re-layouts: 1.87 us -> 2.51 us
where the time goes in v4:
time: 76.1 us; the launch traced here: 75.5 us
  Pallas kernels  73 us (96%)
  local copies, waits for them, and re-layouts  2.51 us (3%)
    pallas_call x1, Pallas kernels, body(): pl.pallas_call(kernel, name='sign_step', out_shape=jax.ShapeDtypeStruct(b...  73 us
    unnamed x7, local copies, waits for them, and re-layouts  2.51 us

profile of v4, /device:TPU:0, one launch (start us, length us, event | category | flops | bytes accessed | tf_op | source)
XLA Modules:
  0.0 75.5 jit_solution(4058093692045695525)
XLA Ops:
  0.0 0.0 copy-start.1
  0.0 0.0 copy-start.2
  0.0 0.7 copy-done.1
  0.7 0.0 copy-done.2
  0.7 0.0 copy-start
  0.7 1.0 %copy-done = bf16[4,1,256,256]{3,2,1,0:T(8,128)(2,1)S(1)} copy-done((bf16[4,1,256,256]{3,2,1,0:T(8,128)(2,1)S(1)}, bf16[4,1,256,256]{3,2,1,0:T(8,128)(2,1)}, u32[]{:S(2)}) %copy-start) | copy-done | bytes 524312
  1.7 73.0 %sign_step.1 = bf16[4,1,256,256]{3,2,1,0:T(8,128)(2,1)S(1)} custom-call(bf16[4,1,256,256]{3,2,1,0:T(8,128)(2,1)S(1)} %copy-done, s32[1,4]{1,0:T(1,128)S(1)} %bitcast.2, s32[1,4]{1,0:T(1,128)S(1)} %bitcast.3), custom_call_target="tpu_custom_call" | custom-call | tf_op jit(solution)/shard_map/sign_step/pallas_call | solution.py:397
  74.7 0.8 %copy.5 = bf16[4,1,256,256]{3,2,1,0:T(8,128)(2,1)} copy(bf16[4,1,256,256]{3,2,1,0:T(8,128)(2,1)S(1)} %sign_step.1) | data formatting | bytes 1048576
Async XLA Ops:
  0.0 0.7 copy-start.1
  0.0 0.7 copy-start.2
  0.7 1.0 %copy-start = (bf16[4,1,256,256]{3,2,1,0:T(8,128)(2,1)S(1)}, bf16[4,1,256,256]{3,2,1,0:T(8,128)(2,1)}, u32[]{:S(2)}) copy-start(bf16[4,1,256,256]{3,2,1,0:T(8,128)(2,1)} %values_in.1) | copy-start | bytes 1572868

commit v5 on v4

v5 whole, which is shorter than its diff:
```python
import functools

import jax
import jax.numpy as jnp
from jax import lax
from jax.experimental import pallas as pl
from jax.experimental.pallas import tpu as pltpu
from jax.sharding import PartitionSpec as P

MESH = pl.DeviceIdType.MESH
BS = 256
ROWS = 4
HEAD = 16
LEFT_PIECES = 4
LEFT_PIECE = ROWS * BS // LEFT_PIECES
LANES = 128
HALVES = BS // LANES
NR = 8
NC = 16


R, S, L, C = "R", "S", "L", "C"
OWN = "own"
MINUS = "m"
PLUS = "p"
SIDE = "side"
TWO = "two"
SIDE_M = "sideM"
SIDE_P = "sideP"
FAR = "far"
HOP = "hop"
SM = "sm"
SP = "sp"
END = "end"
SQUARE = "square"
EVEN = "even"
FINISH = "finish"

PATHS = {
    ("R", "two"): "--+++-++",
    ("R", "far"): "+-+-yy--",
    ("R", "m"): "zzzyzzzz",
    ("R", "p"): "zzzzyzzy",
    ("S", "two"): "----++-+",
    ("S", "far"): "+--yy-+y",
    ("S", "m"): "yzzzzyyz",
    ("S", "p"): "yzyzyyyz",
    ("L", "two"): "+-++",
    ("L", "far"): "-+--",
}

ORDER = (
    (R, OWN, 0),
    (L, OWN, 1),
    (R, OWN, 2),
    (L, HOP, 0),
    (L, OWN, 0),
    (L, HOP, 1),
    (L, HOP, 3),
    (R, OWN, 1),
    (R, OWN, 3),
    (R, SIDE, 0),
    (L, OWN, 3),
    (R, MINUS, 2),
    (R, SIDE, 2),
    (R, OWN, 4),
    (L, MINUS, 0),
    (L, PLUS, 1),
    (R, PLUS, 1),
    (R, SIDE_M, 0),
    (R, OWN, 7),
    (L, SIDE, 0),
    (L, MINUS, 3),
    (R, TWO, 2),
    (R, OWN, 6),
    (L, SIDE, 1),
    (R, OWN, 5),
    (R, PLUS, 0),
    (R, SIDE, 1),
    (L, HOP, 2),
    (L, SIDE, 3),
    (R, SIDE, 3),
    (R, PLUS, 5),
    (R, TWO, 1),
    (R, MINUS, 1),
    (R, PLUS, 7),
    (R, MINUS, 3),
    (R, SIDE_M, 2),
    (L, SP, 0),
    (R, MINUS, 7),
    (R, PLUS, 2),
    (R, SIDE_P, 1),
    (L, PLUS, 0),
    (R, SIDE_P, 0),
    (R, MINUS, 4),
    (R, MINUS, 6),
    (R, SIDE, 6),
    (R, PLUS, 4),
    (L, SP, 3),
    (R, SIDE_P, 3),
    (R, PLUS, 3),
    (L, SM, 1),
    (R, PLUS, 6),
    (R, TWO, 0),
    (L, MINUS, 1),
    (L, SP, 1),
    (L, TWO, 0),
    (L, PLUS, 3),
    (R, SIDE, 7),
    (R, MINUS, 0),
    (L, OWN, 2),
    (R, MINUS, 5),
    (R, TWO, 3),
    (R, SIDE, 5),
    (R, SIDE_P, 7),
    (L, TWO, 1),
    (R, TWO, 5),
    (R, SIDE_M, 1),
    (L, FAR, 0),
    (L, SM, 0),
    (L, TWO, 3),
    (R, FAR, 2),
    (R, FAR, 0),
    (R, SIDE_P, 6),
    (R, SIDE, 4),
    (L, SIDE, 2),
    (L, SM, 3),
    (R, SIDE_P, 2),
    (R, FAR, 3),
    (R, TWO, 4),
    (L, END, 0),
    (R, SIDE_M, 3),
    (R, FAR, 1),
    (L, FAR, 1),
    (C, SQUARE, 0),
    (S, OWN, 0),
    (L, FAR, 3),
    (R, SIDE_P, 4),
    (R, SIDE_M, 6),
    (L, END, 1),
    (R, TWO, 7),
    (C, SQUARE, 1),
    (S, OWN, 1),
    (L, PLUS, 2),
    (L, END, 3),
    (C, SQUARE, 3),
    (S, OWN, 3),
    (R, TWO, 6),
    (L, MINUS, 2),
    (R, FAR, 5),
    (R, SIDE_M, 7),
    (R, FAR, 7),
    (R, SIDE_P, 5),
    (R, FAR, 4),
    (R, SIDE_M, 5),
    (L, SP, 2),
    (R, SIDE_M, 4),
    (S, PLUS, 0),
    (R, FAR, 6),
    (C, SQUARE, 7),
    (C, SQUARE, 5),
    (S, OWN, 5),
    (S, SIDE, 1),
    (S, SIDE, 0),
    (C, SQUARE, 4),
    (S, MINUS, 0),
    (S, OWN, 4),
    (S, TWO, 0),
    (L, TWO, 2),
    (S, PLUS, 1),
    (L, FAR, 2),
    (S, OWN, 7),
    (S, MINUS, 5),
    (L, SM, 2),
    (S, PLUS, 5),
    (L, END, 2),
    (C, SQUARE, 2),
    (S, OWN, 2),
    (S, SIDE_P, 1),
    (C, SQUARE, 6),
    (S, OWN, 6),
    (S, MINUS, 1),
    (S, MINUS, 7),
    (S, MINUS, 4),
    (S, PLUS, 7),
    (S, SIDE_M, 5),
    (S, PLUS, 3),
    (S, PLUS, 2),
    (S, MINUS, 6),
    (S, SIDE, 3),
    (S, PLUS, 4),
    (S, MINUS, 3),
    (S, TWO, 1),
    (S, SIDE_M, 0),
    (S, SIDE_P, 5),
    (S, TWO, 4),
    (S, SIDE, 6),
    (S, SIDE, 4),
    (S, SIDE_P, 2),
    (S, SIDE_P, 0),
    (S, SIDE_M, 1),
    (S, SIDE, 2),
    (S, TWO, 2),
    (S, TWO, 5),
    (S, TWO, 3),
    (S, TWO, 7),
    (S, FAR, 1),
    (S, SIDE, 5),
    (S, SIDE_M, 6),
    (S, SIDE_M, 3),
    (S, PLUS, 6),
    (S, SIDE, 7),
    (S, FAR, 0),
    (C, EVEN, 0),
    (S, SIDE_P, 4),
    (S, SIDE_P, 3),
    (S, FAR, 5),
    (S, FAR, 4),
    (S, SIDE_M, 4),
    (C, EVEN, 1),
    (S, FAR, 3),
    (S, FAR, 2),
    (S, SIDE_M, 2),
    (S, MINUS, 2),
    (C, FINISH, 0),
    (S, FAR, 6),
    (S, FAR, 7),
    (S, TWO, 6),
    (S, SIDE_M, 7),
    (S, SIDE_P, 7),
    (S, SIDE_P, 6),
    (C, FINISH, 1),
)


class Streams:
    def __init__(self, send_sem, recv_sem):
        self.send_sem, self.recv_sem = send_sem, recv_sem
        self.number = {}
        self.started = []

    def copy(self, key, src, dst, device):
        at = self.number.setdefault(key, len(self.number))
        return pltpu.make_async_remote_copy(
            src_ref=src,
            dst_ref=dst,
            send_sem=self.send_sem.at[at],
            recv_sem=self.recv_sem.at[at],
            device_id=device,
            device_id_type=MESH,
        )

    def send(self, key, src, dst, device):
        copy = self.copy(key, src, dst, device)
        copy.start()
        self.started.append(copy)

    def arrived(self, key, dst, device):
        self.copy(key, dst, dst, device).wait_recv()


def kernel(
    values_in, columns_in, live_in, out, values, columns, live, left, right, squared, chosen, cube, in_sem, send_sem, recv_sem
):
    row, col = lax.axis_index("row"), lax.axis_index("col")
    y_lo, z = row // 4, row % 4
    y_hi, x, core = col // 8, (col // 2) % 4, col % 2

    def row_of(dy, dz):
        return ((y_lo + dy) % 2) * 4 + (z + dz + 4) % 4

    def col_of(dy, dx, dc):
        return (((y_hi + dy) % 2) * 4 + (x + dx + 4) % 4) * 2 + (core + dc) % 2

    near = {
        "y": (row_of(1, 0), col),
        "z+": (row_of(0, 1), col),
        "z-": (row_of(0, -1), col),
        "x+": (row, col_of(0, 1, 0)),
        "x-": (row, col_of(0, -1, 0)),
        "h": (row, col_of(1, 0, 0)),
        "c": (row, col_of(0, 0, 1)),
    }
    barrier = pltpu.get_barrier_semaphore()
    for device in near.values():
        pl.semaphore_signal(barrier, inc=1, device_id=device, device_id_type=MESH)

    fetches = [
        pltpu.make_async_copy(source, target, in_sem.at[at])
        for at, (source, target) in enumerate(
            ((columns_in, columns), (live_in, live), (values_in, values))
        )
    ]
    for fetch in fetches:
        fetch.start()
    for fetch in fetches:
        fetch.wait()

    heads = [
        jnp.broadcast_to(columns[0, j].astype(jnp.float32), (1, BS)) for j in range(ROWS)
    ]
    head = jnp.concatenate(
        heads + [jnp.zeros((HEAD - ROWS, BS), jnp.float32)], axis=0
    ).astype(jnp.bfloat16)
    left[col, 0:HEAD, :] = head
    right[row, 0, 0:HEAD, :] = head[:, 0:LANES]
    for j in range(ROWS):
        block = (values[j, 0].astype(jnp.float32) * live[0, j].astype(jnp.float32)).astype(
            jnp.bfloat16
        )
        left[col, HEAD + j * BS : HEAD + (j + 1) * BS, :] = block
        for h in range(HALVES):
            right[row, h, HEAD + j * BS : HEAD + (j + 1) * BS, :] = block[
                :, h * LANES : (h + 1) * LANES
            ]
    pl.semaphore_wait(barrier, len(near))

    streams = Streams(send_sem, recv_sem)

    def piece(buffer, unit, at):
        if buffer is left:
            if at == 0:
                return left.at[unit, pl.ds(0, HEAD + LEFT_PIECE)]
            return left.at[unit, pl.ds(HEAD + at * LEFT_PIECE, LEFT_PIECE)]
        h, j = at // ROWS, at % ROWS
        if buffer is squared:
            return squared.at[unit, h, pl.ds(j * BS, BS)]
        if at == 0:
            return right.at[unit, 0, pl.ds(0, HEAD + BS)]
        return right.at[unit, h, pl.ds(HEAD + j * BS, BS)]

    def send(name, buffer, unit, j, way):
        ref = piece(buffer, unit, j)
        streams.send((name, j, way), ref, ref, near[way])

    def arrived(name, buffer, unit, j, way):
        streams.arrived((name, j, way), piece(buffer, unit, j), near[way])

    def right_step(tag, buffer, name, j):
        two, far, side_m, side_p = (PATHS[tag, k][j] for k in ("two", "far", "m", "p"))
        if name == OWN:
            for way in ("y", "z+", "z-"):
                send(tag + "own", buffer, row, j, way)
        elif name == MINUS:
            arrived(tag + "own", buffer, row_of(0, -1), j, "z+")
            if two == "+":
                send(tag + "two", buffer, row_of(0, -1), j, "z+")
            if side_m == "y":
                send(tag + "sideM", buffer, row_of(0, -1), j, "y")
        elif name == PLUS:
            arrived(tag + "own", buffer, row_of(0, 1), j, "z-")
            if two == "-":
                send(tag + "two", buffer, row_of(0, 1), j, "z-")
            if side_p == "y":
                send(tag + "sideP", buffer, row_of(0, 1), j, "y")
        elif name == SIDE:
            arrived(tag + "own", buffer, row_of(1, 0), j, "y")
            if side_m == "z":
                send(tag + "sideM", buffer, row_of(1, 0), j, "z+")
            if side_p == "z":
                send(tag + "sideP", buffer, row_of(1, 0), j, "z-")
        elif name == TWO:
            arrived(tag + "two", buffer, row_of(0, 2), j, "z" + two)
            if far == "y":
                send(tag + "far", buffer, row_of(0, 2), j, "y")
        elif name == SIDE_M:
            arrived(tag + "sideM", buffer, row_of(1, -1), j, "z+" if side_m == "z" else "y")
            if far == "+":
                send(tag + "far", buffer, row_of(1, -1), j, "z+")
        elif name == SIDE_P:
            arrived(tag + "sideP", buffer, row_of(1, 1), j, "z-" if side_p == "z" else "y")
            if far == "-":
                send(tag + "far", buffer, row_of(1, 1), j, "z-")
        elif name == FAR:
            arrived(tag + "far", buffer, row_of(1, 2), j, "y" if far == "y" else "z" + far)

    def left_step(name, j):
        two, far = (PATHS["L", k][j] for k in ("two", "far"))
        if name == OWN:
            for way in ("x+", "x-", "c"):
                send("Lown", left, col, j, way)
        elif name == HOP:
            send("Lown", left, col, j, "h")
        elif name == MINUS:
            arrived("Lown", left, col_of(0, -1, 0), j, "x+")
            if two == "+":
                send("Ltwo", left, col_of(0, -1, 0), j, "x+")
            send("Lm", left, col_of(0, -1, 0), j, "c")
        elif name == PLUS:
            arrived("Lown", left, col_of(0, 1, 0), j, "x-")
            if two == "-":
                send("Ltwo", left, col_of(0, 1, 0), j, "x-")
            send("Lp", left, col_of(0, 1, 0), j, "c")
        elif name == SIDE:
            arrived("Lown", left, col_of(1, 0, 0), j, "h")
            for way in ("x+", "x-", "c"):
                send("Lside", left, col_of(1, 0, 0), j, way)
        elif name == SM:
            arrived("Lside", left, col_of(1, -1, 0), j, "x+")
            if far == "+":
                send("Lfar", left, col_of(1, -1, 0), j, "x+")
            send("Lsm", left, col_of(1, -1, 0), j, "c")
        elif name == SP:
            arrived("Lside", left, col_of(1, 1, 0), j, "x-")
            if far == "-":
                send("Lfar", left, col_of(1, 1, 0), j, "x-")
            send("Lsp", left, col_of(1, 1, 0), j, "c")
        elif name == TWO:
            arrived("Ltwo", left, col_of(0, 2, 0), j, "x" + two)
            send("Ltwo", left, col_of(0, 2, 0), j, "c")
        elif name == FAR:
            arrived("Lfar", left, col_of(1, 2, 0), j, "x" + far)
            send("Lfar", left, col_of(1, 2, 0), j, "c")
        elif name == END:
            arrived("Lown", left, col_of(0, 0, 1), j, "c")
            arrived("Lm", left, col_of(0, -1, 1), j, "c")
            arrived("Lp", left, col_of(0, 1, 1), j, "c")
            arrived("Lside", left, col_of(1, 0, 1), j, "c")
            arrived("Lsm", left, col_of(1, -1, 1), j, "c")
            arrived("Lsp", left, col_of(1, 1, 1), j, "c")
            arrived("Ltwo", left, col_of(0, 2, 1), j, "c")
            arrived("Lfar", left, col_of(1, 2, 1), j, "c")

    def select(buffer, first, h, i, parts):
        mine = columns[0, i].astype(jnp.float32)
        alive = (live[0, i] > 0).astype(jnp.float32)
        for r in range(NR):
            right_head = right[r, 0, 0:HEAD, :].astype(jnp.float32)
            for part in parts:
                g = 2 * r + part
                own = left[g, 0:HEAD, 0:LANES].astype(jnp.float32)[i : i + 1]
                weights = []
                for b in range(2):
                    met = right_head[2 * part + b : 2 * part + b + 1]
                    weights.append(
                        jnp.where((own == float(b)) & (met == mine), alive, 0.0).astype(
                            jnp.bfloat16
                        )
                    )
                at = first + 2 * part * BS
                chosen[g * BS : (g + 1) * BS, :] = (
                    buffer[r, h, at : at + BS, :] * weights[0]
                    + buffer[r, h, at + BS : at + 2 * BS, :] * weights[1]
                )

    def product(i, parts):
        groups = [2 * r + part for r in range(NR) for part in parts]
        return jnp.dot(
            jnp.concatenate(
                [left[g, HEAD + i * BS : HEAD + (i + 1) * BS, :] for g in groups], axis=1
            ),
            jnp.concatenate([chosen[g * BS : (g + 1) * BS, :] for g in groups], axis=0),
            preferred_element_type=jnp.float32,
        )

    def square(h, i):
        select(right, HEAD, h, i, (0, 1))
        squared[row, h, i * BS : (i + 1) * BS, :] = product(i, (0, 1)).astype(jnp.bfloat16)

    def cube_even(h):
        for i in range(ROWS):
            select(squared, 0, h, i, (0,))
            cube[h, i * BS : (i + 1) * BS, :] = product(i, (0,))

    def finish(h):
        lanes = slice(h * LANES, (h + 1) * LANES)
        for i in range(ROWS):
            select(squared, 0, h, i, (1,))
            cube_part = cube[h, i * BS : (i + 1) * BS, :] + product(i, (1,))
            masked = left[col, HEAD + i * BS : HEAD + (i + 1) * BS, lanes].astype(jnp.float32)
            out[i, 0, :, lanes] = (1.5 * masked - 0.5 * cube_part).astype(jnp.bfloat16)

    for tag, name, j in ORDER:
        if tag == R:
            right_step(tag, right, name, j)
        elif tag == S:
            right_step(tag, squared, name, j)
        elif tag == L:
            left_step(name, j)
        elif name == SQUARE:
            square(j // ROWS, j % ROWS)
        elif name == EVEN:
            cube_even(j)
        else:
            finish(j)
    for copy in streams.started:
        copy.wait_send()


COPIES = 15 * LEFT_PIECES + (7 + 7) * HALVES * ROWS


def body(block_values, block_columns, block_live):
    return pl.pallas_call(
        kernel,
        name="sign_step",
        out_shape=jax.ShapeDtypeStruct(block_values.shape, jnp.bfloat16),
        in_specs=[
            pl.BlockSpec(memory_space=pltpu.HBM),
            pl.BlockSpec(memory_space=pltpu.HBM),
            pl.BlockSpec(memory_space=pltpu.HBM),
        ],
        out_specs=pl.BlockSpec(memory_space=pltpu.VMEM),
        scratch_shapes=[
            pltpu.VMEM(block_values.shape, jnp.bfloat16),
            pltpu.SMEM((1, ROWS), jnp.int32),
            pltpu.SMEM((1, ROWS), jnp.int32),
            pltpu.VMEM((NC, HEAD + ROWS * BS, BS), jnp.bfloat16),
            pltpu.VMEM((NR, HALVES, HEAD + ROWS * BS, LANES), jnp.bfloat16),
            pltpu.VMEM((NR, HALVES, ROWS * BS, LANES), jnp.bfloat16),
            pltpu.VMEM((NC * BS, LANES), jnp.bfloat16),
            pltpu.VMEM((HALVES, ROWS * BS, LANES), jnp.float32),
            pltpu.SemaphoreType.DMA((3,)),
            pltpu.SemaphoreType.DMA((COPIES,)),
            pltpu.SemaphoreType.DMA((COPIES,)),
        ],
        compiler_params=pltpu.CompilerParams(
            collective_id=0, has_side_effects=True, vmem_limit_bytes=28 * 1024 * 1024
        ),
    )(block_values, block_columns.T, block_live.T)


def solution(mesh):
    return jax.shard_map(
        body,
        mesh=mesh,
        in_specs=(P("row", "col", None, None), P("row", "col"), P("row", "col")),
        out_specs=P("row", "col", None, None),
        check_vma=False,
    )
```

time: 76.1 us -> 72.5 us (0.953)
  Pallas kernels: 73 us -> 69.3 us
    pallas_call x1, Pallas kernels: 73 us -> 69.3 us  [body(): pl.pallas_call(kernel, name='sign_step', out_shape=jax.ShapeDtypeStruct(b...]
where the time goes in v5:
time: 72.5 us; the launch traced here: 71.8 us
  Pallas kernels  69.3 us (96%)
  local copies, waits for them, and re-layouts  2.51 us (3%)
    pallas_call x1, Pallas kernels, body(): pl.pallas_call(kernel, name='sign_step', out_shape=jax.ShapeDtypeStruct(b...  69.3 us
    unnamed x7, local copies, waits for them, and re-layouts  2.51 us

profile of v5, /device:TPU:0, one launch (start us, length us, event | category | flops | bytes accessed | tf_op | source)
XLA Modules:
  0.0 71.8 jit_solution(15527800275556886461)
XLA Ops:
  0.0 0.0 copy-start.1
  0.0 0.0 copy-start.2
  0.0 0.7 copy-done.1
  0.7 0.0 copy-done.2
  0.7 0.0 copy-start
  0.7 1.0 %copy-done = bf16[4,1,256,256]{3,2,1,0:T(8,128)(2,1)S(1)} copy-done((bf16[4,1,256,256]{3,2,1,0:T(8,128)(2,1)S(1)}, bf16[4,1,256,256]{3,2,1,0:T(8,128)(2,1)}, u32[]{:S(2)}) %copy-start) | copy-done | bytes 524312
  1.7 69.3 %sign_step.1 = bf16[4,1,256,256]{3,2,1,0:T(8,128)(2,1)S(1)} custom-call(bf16[4,1,256,256]{3,2,1,0:T(8,128)(2,1)S(1)} %copy-done, s32[1,4]{1,0:T(1,128)S(1)} %bitcast.2, s32[1,4]{1,0:T(1,128)S(1)} %bitcast.3), custom_call_target="tpu_custom_call" | custom-call | tf_op jit(solution)/shard_map/sign_step/pallas_call | solution.py:494
  71.0 0.8 %copy.5 = bf16[4,1,256,256]{3,2,1,0:T(8,128)(2,1)} copy(bf16[4,1,256,256]{3,2,1,0:T(8,128)(2,1)S(1)} %sign_step.1) | data formatting | bytes 1048576
Async XLA Ops:
  0.0 0.7 copy-start.1
  0.0 0.7 copy-start.2
  0.7 1.0 %copy-start = (bf16[4,1,256,256]{3,2,1,0:T(8,128)(2,1)S(1)}, bf16[4,1,256,256]{3,2,1,0:T(8,128)(2,1)}, u32[]{:S(2)}) copy-start(bf16[4,1,256,256]{3,2,1,0:T(8,128)(2,1)} %values_in.1) | copy-start | bytes 1572868

commit v6 on v5

--- a/solution.py
+++ b/solution.py
@@ -35,200 +35,202 @@
 SQUARE = "square"
 EVEN = "even"
 FINISH = "finish"
+NEAR = "near"
 
 PATHS = {
-    ("R", "two"): "--+++-++",
-    ("R", "far"): "+-+-yy--",
-    ("R", "m"): "zzzyzzzz",
-    ("R", "p"): "zzzzyzzy",
-    ("S", "two"): "----++-+",
-    ("S", "far"): "+--yy-+y",
-    ("S", "m"): "yzzzzyyz",
+    ("R", "two"): "+-++--+-",
+    ("R", "far"): "-++---y+",
+    ("R", "m"): "zzyzzzzz",
+    ("R", "p"): "zzzzzyyy",
+    ("S", "two"): "-+---+-+",
+    ("S", "far"): "+y+--y+-",
+    ("S", "m"): "zzyyzyzy",
     ("S", "p"): "yzyzyyyz",
-    ("L", "two"): "+-++",
-    ("L", "far"): "-+--",
+    ("L", "two"): "+--+",
+    ("L", "far"): "-++-",
 }
 
 ORDER = (
-    (R, OWN, 0),
-    (L, OWN, 1),
-    (R, OWN, 2),
-    (L, HOP, 0),
-    (L, OWN, 0),
-    (L, HOP, 1),
-    (L, HOP, 3),
     (R, OWN, 1),
     (R, OWN, 3),
-    (R, SIDE, 0),
-    (L, OWN, 3),
+    (L, OWN, 0),
+    (L, HOP, 0),
+    (R, OWN, 0),
+    (R, OWN, 4),
+    (L, OWN, 1),
+    (R, SIDE, 1),
+    (R, PLUS, 1),
+    (L, HOP, 1),
+    (L, OWN, 2),
+    (L, MINUS, 0),
+    (L, HOP, 2),
+    (R, OWN, 2),
+    (R, SIDE, 3),
+    (R, MINUS, 3),
+    (R, MINUS, 0),
+    (R, PLUS, 3),
+    (L, SIDE, 0),
+    (R, OWN, 7),
     (R, MINUS, 2),
-    (R, SIDE, 2),
-    (R, OWN, 4),
-    (L, MINUS, 0),
-    (L, PLUS, 1),
-    (R, PLUS, 1),
-    (R, SIDE_M, 0),
-    (R, OWN, 7),
-    (L, SIDE, 0),
-    (L, MINUS, 3),
-    (R, TWO, 2),
+    (R, PLUS, 4),
+    (L, HOP, 3),
     (R, OWN, 6),
-    (L, SIDE, 1),
     (R, OWN, 5),
     (R, PLUS, 0),
-    (R, SIDE, 1),
-    (L, HOP, 2),
+    (L, PLUS, 1),
+    (L, SIDE, 1),
+    (L, TWO, 0),
+    (R, SIDE_P, 3),
+    (R, SIDE, 0),
+    (L, PLUS, 2),
+    (L, SP, 0),
+    (L, PLUS, 0),
+    (L, MINUS, 1),
+    (R, SIDE, 2),
+    (L, SIDE, 2),
+    (R, MINUS, 6),
+    (R, TWO, 3),
+    (R, SIDE_M, 1),
+    (L, TWO, 1),
+    (R, TWO, 1),
+    (R, SIDE_M, 2),
+    (L, SM, 1),
+    (R, SIDE, 7),
+    (R, SIDE, 4),
+    (R, PLUS, 5),
+    (R, TWO, 2),
+    (R, MINUS, 5),
+    (L, SP, 1),
+    (R, SIDE_P, 0),
+    (R, SIDE_M, 3),
+    (L, SM, 2),
+    (L, MINUS, 2),
+    (R, PLUS, 7),
+    (L, OWN, 3),
+    (L, FAR, 0),
+    (R, SIDE_P, 4),
+    (R, MINUS, 7),
+    (L, SM, 0),
+    (R, FAR, 1),
+    (R, TWO, 6),
+    (R, MINUS, 4),
+    (R, TWO, 4),
+    (L, TWO, 2),
+    (R, SIDE, 5),
+    (R, SIDE, 6),
+    (R, SIDE_P, 5),
+    (R, MINUS, 1),
+    (R, SIDE_P, 2),
+    (R, TWO, 0),
     (L, SIDE, 3),
-    (R, SIDE, 3),
-    (R, PLUS, 5),
-    (R, TWO, 1),
-    (R, MINUS, 1),
-    (R, PLUS, 7),
-    (R, MINUS, 3),
-    (R, SIDE_M, 2),
-    (L, SP, 0),
-    (R, MINUS, 7),
+    (R, FAR, 3),
+    (R, PLUS, 6),
+    (R, FAR, 0),
     (R, PLUS, 2),
+    (L, END, 0),
+    (R, SIDE_M, 7),
     (R, SIDE_P, 1),
-    (L, PLUS, 0),
-    (R, SIDE_P, 0),
-    (R, MINUS, 4),
-    (R, MINUS, 6),
-    (R, SIDE, 6),
-    (R, PLUS, 4),
-    (L, SP, 3),
-    (R, SIDE_P, 3),
-    (R, PLUS, 3),
-    (L, SM, 1),
-    (R, PLUS, 6),
-    (R, TWO, 0),
-    (L, MINUS, 1),
-    (L, SP, 1),
-    (L, TWO, 0),
-    (L, PLUS, 3),
-    (R, SIDE, 7),
-    (R, MINUS, 0),
-    (L, OWN, 2),
-    (R, MINUS, 5),
-    (R, TWO, 3),
-    (R, SIDE, 5),
-    (R, SIDE_P, 7),
-    (L, TWO, 1),
-    (R, TWO, 5),
-    (R, SIDE_M, 1),
-    (L, FAR, 0),
-    (L, SM, 0),
-    (L, TWO, 3),
+    (L, FAR, 1),
     (R, FAR, 2),
-    (R, FAR, 0),
-    (R, SIDE_P, 6),
-    (R, SIDE, 4),
-    (L, SIDE, 2),
-    (L, SM, 3),
-    (R, SIDE_P, 2),
-    (R, FAR, 3),
-    (R, TWO, 4),
-    (L, END, 0),
-    (R, SIDE_M, 3),
-    (R, FAR, 1),
-    (L, FAR, 1),
+    (L, SP, 2),
+    (R, SIDE_M, 0),
     (C, SQUARE, 0),
     (S, OWN, 0),
-    (L, FAR, 3),
-    (R, SIDE_P, 4),
-    (R, SIDE_M, 6),
     (L, END, 1),
-    (R, TWO, 7),
+    (L, FAR, 2),
+    (R, SIDE_P, 7),
     (C, SQUARE, 1),
     (S, OWN, 1),
-    (L, PLUS, 2),
+    (L, END, 2),
+    (C, SQUARE, 2),
+    (R, TWO, 5),
+    (S, OWN, 2),
+    (R, FAR, 4),
+    (R, SIDE_M, 5),
+    (R, FAR, 5),
+    (R, TWO, 7),
+    (L, MINUS, 3),
+    (S, PLUS, 0),
+    (R, SIDE_P, 6),
+    (L, PLUS, 3),
+    (R, SIDE_M, 6),
+    (R, FAR, 6),
+    (R, FAR, 7),
+    (L, SP, 3),
+    (R, SIDE_M, 4),
+    (C, SQUARE, 4),
+    (S, OWN, 4),
+    (C, SQUARE, 5),
+    (C, SQUARE, 6),
+    (L, SM, 3),
+    (S, OWN, 6),
+    (S, OWN, 5),
+    (S, SIDE, 0),
+    (S, MINUS, 2),
+    (S, PLUS, 2),
+    (S, SIDE, 1),
+    (L, TWO, 3),
+    (S, MINUS, 1),
+    (L, FAR, 3),
     (L, END, 3),
     (C, SQUARE, 3),
     (S, OWN, 3),
-    (R, TWO, 6),
-    (L, MINUS, 2),
-    (R, FAR, 5),
-    (R, SIDE_M, 7),
-    (R, FAR, 7),
-    (R, SIDE_P, 5),
-    (R, FAR, 4),
-    (R, SIDE_M, 5),
-    (L, SP, 2),
-    (R, SIDE_M, 4),
-    (S, PLUS, 0),
-    (R, FAR, 6),
     (C, SQUARE, 7),
-    (C, SQUARE, 5),
-    (S, OWN, 5),
-    (S, SIDE, 1),
-    (S, SIDE, 0),
-    (C, SQUARE, 4),
+    (S, OWN, 7),
+    (S, PLUS, 4),
+    (S, SIDE_M, 1),
+    (S, SIDE, 5),
+    (S, TWO, 0),
+    (S, MINUS, 5),
+    (S, SIDE_M, 0),
+    (S, TWO, 1),
+    (S, SIDE, 3),
     (S, MINUS, 0),
-    (S, OWN, 4),
-    (S, TWO, 0),
-    (L, TWO, 2),
+    (S, SIDE, 7),
+    (S, PLUS, 5),
+    (S, MINUS, 3),
+    (S, SIDE, 6),
+    (S, PLUS, 3),
+    (S, TWO, 4),
+    (S, TWO, 5),
+    (S, SIDE_M, 5),
+    (S, SIDE_M, 2),
+    (S, SIDE, 4),
+    (S, SIDE_P, 1),
+    (S, SIDE_P, 3),
+    (S, SIDE_P, 4),
     (S, PLUS, 1),
-    (L, FAR, 2),
-    (S, OWN, 7),
-    (S, MINUS, 5),
-    (L, SM, 2),
-    (S, PLUS, 5),
-    (L, END, 2),
-    (C, SQUARE, 2),
-    (S, OWN, 2),
-    (S, SIDE_P, 1),
-    (C, SQUARE, 6),
-    (S, OWN, 6),
-    (S, MINUS, 1),
-    (S, MINUS, 7),
+    (S, SIDE_P, 0),
+    (S, PLUS, 7),
     (S, MINUS, 4),
-    (S, PLUS, 7),
-    (S, SIDE_M, 5),
-    (S, PLUS, 3),
-    (S, PLUS, 2),
-    (S, MINUS, 6),
-    (S, SIDE, 3),
-    (S, PLUS, 4),
-    (S, MINUS, 3),
-    (S, TWO, 1),
-    (S, SIDE_M, 0),
-    (S, SIDE_P, 5),
-    (S, TWO, 4),
-    (S, SIDE, 6),
-    (S, SIDE, 4),
     (S, SIDE_P, 2),
-    (S, SIDE_P, 0),
-    (S, SIDE_M, 1),
-    (S, SIDE, 2),
-    (S, TWO, 2),
-    (S, TWO, 5),
-    (S, TWO, 3),
-    (S, TWO, 7),
     (S, FAR, 1),
-    (S, SIDE, 5),
-    (S, SIDE_M, 6),
-    (S, SIDE_M, 3),
-    (S, PLUS, 6),
-    (S, SIDE, 7),
     (S, FAR, 0),
     (C, EVEN, 0),
-    (S, SIDE_P, 4),
-    (S, SIDE_P, 3),
+    (S, PLUS, 6),
+    (S, MINUS, 7),
+    (S, SIDE_M, 6),
+    (S, SIDE_P, 5),
+    (S, MINUS, 6),
+    (S, FAR, 2),
+    (S, TWO, 2),
+    (S, SIDE_P, 7),
+    (S, SIDE_M, 3),
+    (S, TWO, 3),
+    (S, SIDE, 2),
+    (S, FAR, 3),
+    (C, FINISH, 0),
     (S, FAR, 5),
     (S, FAR, 4),
     (S, SIDE_M, 4),
     (C, EVEN, 1),
-    (S, FAR, 3),
-    (S, FAR, 2),
-    (S, SIDE_M, 2),
-    (S, MINUS, 2),
-    (C, FINISH, 0),
+    (C, NEAR, 1),
+    (S, TWO, 7),
+    (S, TWO, 6),
+    (S, SIDE_P, 6),
+    (S, SIDE_M, 7),
     (S, FAR, 6),
     (S, FAR, 7),
-    (S, TWO, 6),
-    (S, SIDE_M, 7),
-    (S, SIDE_P, 7),
-    (S, SIDE_P, 6),
     (C, FINISH, 1),
 )
 
@@ -304,15 +306,20 @@
     ).astype(jnp.bfloat16)
     left[col, 0:HEAD, :] = head
     right[row, 0, 0:HEAD, :] = head[:, 0:LANES]
+
+    def masked_block(j, lanes):
+        block = values[j, 0, :, lanes].astype(jnp.float32) * live[0, j].astype(jnp.float32)
+        return block.astype(jnp.bfloat16)
+
+    def build_right(h, j):
+        lanes = slice(h * LANES, (h + 1) * LANES)
+        right[row, h, HEAD + j * BS : HEAD + (j + 1) * BS, :] = masked_block(j, lanes)
+
+    def build_left(j):
+        left[col, HEAD + j * BS : HEAD + (j + 1) * BS, :] = masked_block(j, slice(None))
+
     for j in range(ROWS):
-        block = (values[j, 0].astype(jnp.float32) * live[0, j].astype(jnp.float32)).astype(
-            jnp.bfloat16
-        )
-        left[col, HEAD + j * BS : HEAD + (j + 1) * BS, :] = block
-        for h in range(HALVES):
-            right[row, h, HEAD + j * BS : HEAD + (j + 1) * BS, :] = block[
-                :, h * LANES : (h + 1) * LANES
-            ]
+        build_right(0, j)
     pl.semaphore_wait(barrier, len(near))
 
     streams = Streams(send_sem, recv_sem)
@@ -339,6 +346,8 @@
     def right_step(tag, buffer, name, j):
         two, far, side_m, side_p = (PATHS[tag, k][j] for k in ("two", "far", "m", "p"))
         if name == OWN:
+            if tag == R and j >= ROWS:
+                build_right(1, j - ROWS)
             for way in ("y", "z+", "z-"):
                 send(tag + "own", buffer, row, j, way)
         elif name == MINUS:
@@ -374,8 +383,13 @@
         elif name == FAR:
             arrived(tag + "far", buffer, row_of(1, 2), j, "y" if far == "y" else "z" + far)
 
+    built = set()
+
     def left_step(name, j):
         two, far = (PATHS["L", k][j] for k in ("two", "far"))
+        if name in (OWN, HOP) and j not in built:
+            built.add(j)
+            build_left(j)
         if name == OWN:
             for way in ("x+", "x-", "c"):
                 send("Lown", left, col, j, way)
@@ -421,52 +435,63 @@
             arrived("Ltwo", left, col_of(0, 2, 1), j, "c")
             arrived("Lfar", left, col_of(1, 2, 1), j, "c")
 
-    def select(buffer, first, h, i, parts):
+    def select(buffer, first, h, i, groups):
         mine = columns[0, i].astype(jnp.float32)
         alive = (live[0, i] > 0).astype(jnp.float32)
-        for r in range(NR):
+        for slot, (r, part) in enumerate(groups):
             right_head = right[r, 0, 0:HEAD, :].astype(jnp.float32)
-            for part in parts:
-                g = 2 * r + part
-                own = left[g, 0:HEAD, 0:LANES].astype(jnp.float32)[i : i + 1]
-                weights = []
-                for b in range(2):
-                    met = right_head[2 * part + b : 2 * part + b + 1]
-                    weights.append(
-                        jnp.where((own == float(b)) & (met == mine), alive, 0.0).astype(
-                            jnp.bfloat16
-                        )
-                    )
-                at = first + 2 * part * BS
-                chosen[g * BS : (g + 1) * BS, :] = (
-                    buffer[r, h, at : at + BS, :] * weights[0]
-                    + buffer[r, h, at + BS : at + 2 * BS, :] * weights[1]
+            own = left[2 * r + part, 0:HEAD, 0:LANES].astype(jnp.float32)[i : i + 1]
+            weights = []
+            for b in range(2):
+                met = right_head[2 * part + b : 2 * part + b + 1]
+                weights.append(
+                    jnp.where((own == float(b)) & (met == mine), alive, 0.0).astype(jnp.bfloat16)
                 )
-
-    def product(i, parts):
-        groups = [2 * r + part for r in range(NR) for part in parts]
+            at = first + 2 * part * BS
+            chosen[slot * BS : (slot + 1) * BS, :] = (
+                buffer[r, h, at : at + BS, :] * weights[0]
+                + buffer[r, h, at + BS : at + 2 * BS, :] * weights[1]
+            )
+
+    def product(i, groups):
         return jnp.dot(
             jnp.concatenate(
-                [left[g, HEAD + i * BS : HEAD + (i + 1) * BS, :] for g in groups], axis=1
+                [
+                    left[2 * r + part, HEAD + i * BS : HEAD + (i + 1) * BS, :]
+                    for r, part in groups
+                ],
+                axis=1,
             ),
-            jnp.concatenate([chosen[g * BS : (g + 1) * BS, :] for g in groups], axis=0),
+            chosen[0 : len(groups) * BS, :],
             preferred_element_type=jnp.float32,
         )
 
+    both = [(r, part) for r in range(NR) for part in range(2)]
+    even = [(r, 0) for r in range(NR)]
+    odd = [(r, 1) for r in range(NR)]
+    odd_near = [(row_of(dy, dz), 1) for dy, dz in ((0, 0), (1, 0), (0, -1), (0, 1))]
+    odd_far = [(row_of(dy, dz), 1) for dy, dz in ((0, 2), (1, -1), (1, 1), (1, 2))]
+
     def square(h, i):
-        select(right, HEAD, h, i, (0, 1))
-        squared[row, h, i * BS : (i + 1) * BS, :] = product(i, (0, 1)).astype(jnp.bfloat16)
+        select(right, HEAD, h, i, both)
+        squared[row, h, i * BS : (i + 1) * BS, :] = product(i, both).astype(jnp.bfloat16)
 
     def cube_even(h):
         for i in range(ROWS):
-            select(squared, 0, h, i, (0,))
-            cube[h, i * BS : (i + 1) * BS, :] = product(i, (0,))
+            select(squared, 0, h, i, even)
+            cube[h, i * BS : (i + 1) * BS, :] = product(i, even)
+
+    def cube_near(h):
+        for i in range(ROWS):
+            select(squared, 0, h, i, odd_near)
+            cube[h, i * BS : (i + 1) * BS, :] += product(i, odd_near)
 
     def finish(h):
+        groups = odd_far if h == HALVES - 1 else odd
         lanes = slice(h * LANES, (h + 1) * LANES)
         for i in range(ROWS):
-            select(squared, 0, h, i, (1,))
-            cube_part = cube[h, i * BS : (i + 1) * BS, :] + product(i, (1,))
+            select(squared, 0, h, i, groups)
+            cube_part = cube[h, i * BS : (i + 1) * BS, :] + product(i, groups)
             masked = left[col, HEAD + i * BS : HEAD + (i + 1) * BS, lanes].astype(jnp.float32)
             out[i, 0, :, lanes] = (1.5 * masked - 0.5 * cube_part).astype(jnp.bfloat16)
 
@@ -481,6 +506,8 @@
             square(j // ROWS, j % ROWS)
         elif name == EVEN:
             cube_even(j)
+        elif name == NEAR:
+            cube_near(j)
         else:
             finish(j)
     for copy in streams.started:

time: 72.5 us -> 71.6 us (0.988)
  no operation moved by 1% of the time
where the time goes in v6:
time: 71.6 us; the launch traced here: 71.2 us
  Pallas kernels  68.6 us (96%)
  local copies, waits for them, and re-layouts  2.51 us (4%)
    pallas_call x1, Pallas kernels, body(): pl.pallas_call(kernel, name='sign_step', out_shape=jax.ShapeDtypeStruct(b...  68.6 us
    unnamed x7, local copies, waits for them, and re-layouts  2.51 us

profile of v6, /device:TPU:0, one launch (start us, length us, event | category | flops | bytes accessed | tf_op | source)
XLA Modules:
  0.0 71.2 jit_solution(2927540436904201552)
XLA Ops:
  0.0 0.0 copy-start.1
  0.0 0.0 copy-start.2
  0.0 0.7 copy-done.1
  0.7 0.0 copy-done.2
  0.7 0.0 copy-start
  0.7 1.0 %copy-done = bf16[4,1,256,256]{3,2,1,0:T(8,128)(2,1)S(1)} copy-done((bf16[4,1,256,256]{3,2,1,0:T(8,128)(2,1)S(1)}, bf16[4,1,256,256]{3,2,1,0:T(8,128)(2,1)}, u32[]{:S(2)}) %copy-start) | copy-done | bytes 524312
  1.7 68.6 %sign_step.1 = bf16[4,1,256,256]{3,2,1,0:T(8,128)(2,1)S(1)} custom-call(bf16[4,1,256,256]{3,2,1,0:T(8,128)(2,1)S(1)} %copy-done, s32[1,4]{1,0:T(1,128)S(1)} %bitcast.2, s32[1,4]{1,0:T(1,128)S(1)} %bitcast.3), custom_call_target="tpu_custom_call" | custom-call | tf_op jit(solution)/shard_map/sign_step/pallas_call | solution.py:521
  70.4 0.8 %copy.5 = bf16[4,1,256,256]{3,2,1,0:T(8,128)(2,1)} copy(bf16[4,1,256,256]{3,2,1,0:T(8,128)(2,1)S(1)} %sign_step.1) | data formatting | bytes 1048576
Async XLA Ops:
  0.0 0.7 copy-start.1
  0.0 0.7 copy-start.2
  0.7 1.0 %copy-start = (bf16[4,1,256,256]{3,2,1,0:T(8,128)(2,1)S(1)}, bf16[4,1,256,256]{3,2,1,0:T(8,128)(2,1)}, u32[]{:S(2)}) copy-start(bf16[4,1,256,256]{3,2,1,0:T(8,128)(2,1)} %values_in.1) | copy-start | bytes 1572868

commit v7 on v6

--- a/solution.py
+++ b/solution.py
@@ -290,12 +290,13 @@
     fetches = [
         pltpu.make_async_copy(source, target, in_sem.at[at])
         for at, (source, target) in enumerate(
-            ((columns_in, columns), (live_in, live), (values_in, values))
+            [(columns_in, columns), (live_in, live)]
+            + [(values_in.at[j], values.at[j]) for j in range(ROWS)]
         )
     ]
     for fetch in fetches:
         fetch.start()
-    for fetch in fetches:
+    for fetch in fetches[:2]:
         fetch.wait()
 
     heads = [
@@ -319,6 +320,7 @@
         left[col, HEAD + j * BS : HEAD + (j + 1) * BS, :] = masked_block(j, slice(None))
 
     for j in range(ROWS):
+        fetches[2 + j].wait()
         build_right(0, j)
     pl.semaphore_wait(barrier, len(near))
 
@@ -537,7 +539,7 @@
             pltpu.VMEM((NR, HALVES, ROWS * BS, LANES), jnp.bfloat16),
             pltpu.VMEM((NC * BS, LANES), jnp.bfloat16),
             pltpu.VMEM((HALVES, ROWS * BS, LANES), jnp.float32),
-            pltpu.SemaphoreType.DMA((3,)),
+            pltpu.SemaphoreType.DMA((2 + ROWS,)),
             pltpu.SemaphoreType.DMA((COPIES,)),
             pltpu.SemaphoreType.DMA((COPIES,)),
         ],

time: 71.6 us -> 71.6 us (level)
  no operation moved by 1% of the time
where the time goes in v7:
time: 71.6 us; the launch traced here: 71.2 us
  Pallas kernels  68.7 us (96%)
  local copies, waits for them, and re-layouts  2.51 us (4%)
    pallas_call x1, Pallas kernels, body(): pl.pallas_call(kernel, name='sign_step', out_shape=jax.ShapeDtypeStruct(b...  68.7 us
    unnamed x7, local copies, waits for them, and re-layouts  2.51 us

profile of v7, /device:TPU:0, one launch (start us, length us, event | category | flops | bytes accessed | tf_op | source)
XLA Modules:
  0.0 71.2 jit_solution(2041167262226938086)
XLA Ops:
  0.0 0.0 copy-start.1
  0.0 0.0 copy-start.2
  0.0 0.7 copy-done.1
  0.7 0.0 copy-done.2
  0.7 0.0 copy-start
  0.7 1.0 %copy-done = bf16[4,1,256,256]{3,2,1,0:T(8,128)(2,1)S(1)} copy-done((bf16[4,1,256,256]{3,2,1,0:T(8,128)(2,1)S(1)}, bf16[4,1,256,256]{3,2,1,0:T(8,128)(2,1)}, u32[]{:S(2)}) %copy-start) | copy-done | bytes 524312
  1.7 68.7 %sign_step.1 = bf16[4,1,256,256]{3,2,1,0:T(8,128)(2,1)S(1)} custom-call(bf16[4,1,256,256]{3,2,1,0:T(8,128)(2,1)S(1)} %copy-done, s32[1,4]{1,0:T(1,128)S(1)} %bitcast.2, s32[1,4]{1,0:T(1,128)S(1)} %bitcast.3), custom_call_target="tpu_custom_call" | custom-call | tf_op jit(solution)/shard_map/sign_step/pallas_call | solution.py:523
  70.4 0.8 %copy.5 = bf16[4,1,256,256]{3,2,1,0:T(8,128)(2,1)} copy(bf16[4,1,256,256]{3,2,1,0:T(8,128)(2,1)S(1)} %sign_step.1) | data formatting | bytes 1048576
Async XLA Ops:
  0.0 0.7 copy-start.1
  0.0 0.7 copy-start.2
  0.7 1.0 %copy-start = (bf16[4,1,256,256]{3,2,1,0:T(8,128)(2,1)S(1)}, bf16[4,1,256,256]{3,2,1,0:T(8,128)(2,1)}, u32[]{:S(2)}) copy-start(bf16[4,1,256,256]{3,2,1,0:T(8,128)(2,1)} %values_in.1) | copy-start | bytes 1572868

commit v8 on v7

--- a/solution.py
+++ b/solution.py
@@ -350,7 +350,7 @@
         if name == OWN:
             if tag == R and j >= ROWS:
                 build_right(1, j - ROWS)
-            for way in ("y", "z+", "z-"):
+            for way in ("z+", "z-", "y"):
                 send(tag + "own", buffer, row, j, way)
         elif name == MINUS:
             arrived(tag + "own", buffer, row_of(0, -1), j, "z+")

time: 71.6 us -> 71.6 us (level)
  no operation moved by 1% of the time
where the time goes in v8:
time: 71.6 us; the launch traced here: 71.2 us
  Pallas kernels  68.7 us (96%)
  local copies, waits for them, and re-layouts  2.51 us (4%)
    pallas_call x1, Pallas kernels, body(): pl.pallas_call(kernel, name='sign_step', out_shape=jax.ShapeDtypeStruct(b...  68.7 us
    unnamed x7, local copies, waits for them, and re-layouts  2.51 us

profile of v8, /device:TPU:0, one launch (start us, length us, event | category | flops | bytes accessed | tf_op | source)
XLA Modules:
  0.0 71.2 jit_solution(14629854572950123008)
XLA Ops:
  0.0 0.0 copy-start.1
  0.0 0.0 copy-start.2
  0.0 0.7 copy-done.1
  0.7 0.0 copy-done.2
  0.7 0.0 copy-start
  0.7 1.0 %copy-done = bf16[4,1,256,256]{3,2,1,0:T(8,128)(2,1)S(1)} copy-done((bf16[4,1,256,256]{3,2,1,0:T(8,128)(2,1)S(1)}, bf16[4,1,256,256]{3,2,1,0:T(8,128)(2,1)}, u32[]{:S(2)}) %copy-start) | copy-done | bytes 524312
  1.7 68.7 %sign_step.1 = bf16[4,1,256,256]{3,2,1,0:T(8,128)(2,1)S(1)} custom-call(bf16[4,1,256,256]{3,2,1,0:T(8,128)(2,1)S(1)} %copy-done, s32[1,4]{1,0:T(1,128)S(1)} %bitcast.2, s32[1,4]{1,0:T(1,128)S(1)} %bitcast.3), custom_call_target="tpu_custom_call" | custom-call | tf_op jit(solution)/shard_map/sign_step/pallas_call | solution.py:523
  70.4 0.8 %copy.5 = bf16[4,1,256,256]{3,2,1,0:T(8,128)(2,1)} copy(bf16[4,1,256,256]{3,2,1,0:T(8,128)(2,1)S(1)} %sign_step.1) | data formatting | bytes 1048576
Async XLA Ops:
  0.0 0.7 copy-start.1
  0.0 0.7 copy-start.2
  0.7 1.0 %copy-start = (bf16[4,1,256,256]{3,2,1,0:T(8,128)(2,1)S(1)}, bf16[4,1,256,256]{3,2,1,0:T(8,128)(2,1)}, u32[]{:S(2)}) copy-start(bf16[4,1,256,256]{3,2,1,0:T(8,128)(2,1)} %values_in.1) | copy-start | bytes 1572868
